TPU v7x, 256 devices: a whole 4x4x8 slice. The times are simulated.
256 devices in a mesh: stream: 32 (over z, y), item: 8 (over x, core).
Axes of the slice: x: 4, y: 4, z: 8, core: 2. Of those that a mesh axis runs over, the one named last changes fastest.
Arguments:
- event_items: int32 [131072], P('stream'), may hold values from 0 to 262143, as said below
- event_sessions: int32 [131072], P('stream'), may hold values from 0 to 8191, never falling along the last dimension, each value on 1 to 64 neighbouring positions
- sketch_bits: int32 [15, 262144], P(None, 'item'), may hold values from 0 to 262143
Outputs:
- sketch: float32 [128, 256], P('stream')
Inputs may be any that keep to these rules, and one draw needn't show every extreme that they name: `event_items`: item 262144 - 1 occurs at least once.
All inputs are finite; a program needn't handle non-finite values.
Results may differ from a plain program's by a relative error of at most 0.0006.
Values may be sent and summed in bfloat16 or wider, within the bound.
No kernel may reach another device: no remote copies, remote signals or barrier semaphores. Data moves between devices by JAX's collectives and lax.ppermute only.
A program may use at most 128 MiB of HBM per device.

v0:
```python
import math

import jax
import jax.numpy as jnp
from jax import lax
from jax.sharding import PartitionSpec as P

SKETCH = 256
WINDOW = 15
ROWS_DEV = 4


def with_halo(shard, sides, width):
    for axis, dim in sides:
        devices, length = (lax.axis_size(axis), shard.shape[dim])
        up = [(i, (i + 1) % devices) for i in range(devices - 1)]
        down = [(j, i) for i, j in up]
        last = lax.slice_in_dim(shard, length - width, length, axis=dim)
        first = lax.slice_in_dim(shard, 0, width, axis=dim)
        before = lax.ppermute(last, axis, up)
        after = lax.ppermute(first, axis, down)
        shard = jnp.concatenate([before, shard, after], axis=dim)
    return shard


def pointwise(count_block, row_margin, col_margin, pair_total):
    log_ratio = (
        jnp.log(jnp.maximum(count_block, 1.0))
        + jnp.log(pair_total)
        - jnp.log(jnp.maximum(row_margin, 1.0))
        - jnp.log(jnp.maximum(col_margin, 1.0))
    )
    return jnp.where(count_block > 0, jnp.maximum(log_ratio, 0.0), 0.0)


def sign_table(bit_block, sketch_width):
    word_count = bit_block.shape[0]
    spread = jnp.repeat(bit_block, 18, axis=0, total_repeat_length=word_count * 18)[:sketch_width]
    bit_shift = (jnp.arange(sketch_width, dtype=jnp.int32) % 18)[:, None]
    return (2 * jnp.bitwise_and(jnp.right_shift(spread, bit_shift), 1) - 1).astype(jnp.float32)


def slab_pairs(ext_items, ext_sessions, row_items):
    extent = ext_items.shape[0]
    own_count = extent - 2 * WINDOW
    own_sessions = ext_sessions[WINDOW : WINDOW + own_count]
    own_items = ext_items[WINDOW : WINDOW + own_count]
    offset = (
        lax.broadcasted_iota(jnp.int32, (own_count, extent), 1)
        - lax.broadcasted_iota(jnp.int32, (own_count, extent), 0)
        - WINDOW
    )
    nearby = (jnp.abs(offset) <= WINDOW) & (offset != 0)
    same_session = own_sessions[:, None] == ext_sessions[None, :]
    banded = (nearby & same_session).astype(jnp.bfloat16)
    row_hot = (
        own_items[None, :] == lax.broadcasted_iota(jnp.int32, (row_items, own_count), 0)
    ).astype(jnp.bfloat16)
    pair_links = lax.dot_general(
        banded, row_hot, (((0,), (1,)), ((), ())), preferred_element_type=jnp.float32
    )
    weights = jnp.sum(banded, axis=0, dtype=jnp.float32)
    return (pair_links, weights)


def tile_block(links_float, ext_items, first_id, col_count):
    local_ids = ext_items - first_id
    in_band = (local_ids >= 0) & (local_ids < col_count)
    return jax.ops.segment_sum(
        jnp.where(in_band[:, None], links_float, 0.0),
        jnp.where(in_band, local_ids, 0),
        num_segments=col_count,
    )


def band_counts(weights, ext_items, first_id, col_count):
    local_ids = ext_items - first_id
    in_band = (local_ids >= 0) & (local_ids < col_count)
    return jax.ops.segment_sum(
        jnp.where(in_band, weights, 0.0), jnp.where(in_band, local_ids, 0), num_segments=col_count
    )


def local(event_items, event_sessions, sketch_bits):
    slab_count = lax.axis_size("stream")
    band_size = sketch_bits.shape[1]
    owned_cols = band_size // slab_count
    row_items = ROWS_DEV * slab_count
    band_start = lax.axis_index("item") * band_size
    own_start = lax.axis_index("stream") * owned_cols
    total_events = event_items.shape[0] * slab_count
    stacked = jnp.stack([event_items, event_sessions + 1])
    extended = with_halo(stacked, (("stream", 1),), WINDOW)
    pair_links, weights = slab_pairs(extended[0], extended[1], row_items)
    band_margin = band_counts(weights, extended[0], band_start, band_size)
    count_tile = lax.psum_scatter(
        tile_block(
            pair_links, extended[0], band_start, owned_cols * lax.axis_size("stream")
        ).astype(jnp.bfloat16),
        "stream",
        scatter_dimension=0,
        tiled=True,
    ).astype(jnp.float32)
    col_margin = lax.psum_scatter(
        band_margin.astype(jnp.bfloat16), "stream", scatter_dimension=0, tiled=True
    ).astype(jnp.float32)
    row_margin, pair_total = lax.psum(
        (jnp.sum(count_tile, axis=0), jnp.sum(col_margin)), ("stream", "item")
    )
    own_bits = lax.dynamic_slice_in_dim(sketch_bits, own_start, owned_cols, 1)
    sign_rows = sign_table(own_bits, SKETCH)
    positive = pointwise(count_tile, row_margin[None, :], col_margin[:, None], pair_total)
    partial_value = lax.dot_general(
        positive,
        sign_rows,
        (((0,), (1,)), ((), ())),
        precision=lax.Precision.HIGHEST,
        preferred_element_type=jnp.float32,
    )
    summed = lax.psum(partial_value, ("stream", "item"))
    own_rows = lax.dynamic_slice_in_dim(summed, lax.axis_index("stream") * ROWS_DEV, ROWS_DEV, 0)
    return own_rows / math.sqrt(total_events)


def solution(mesh):
    placed = (P("stream"), P("stream"), P(None, "item"))
    return jax.shard_map(
        local, mesh=mesh, in_specs=placed, out_specs=P("stream", None), check_vma=False
    )
```

profile of v0, /device:TPU:1, one launch (start us, length us, event | category | flops | bytes accessed | tf_op | source)
XLA Modules:
  0.0 782.3 jit_solution(2511389435921532583)
XLA Ops:
  6.5 0.0 copy-start
  6.5 0.0 all-reduce.7.cloned.1.call-start
  6.5 0.9 broadcast_add_fusion
  7.4 0.7 fusion.38
  8.2 4.0 collective-permute-start
  12.2 1.3 collective-permute-start.1
  13.5 0.7 pad_add_fusion
  14.2 1.0 iota_compare_fusion.5
  15.3 0.0 collective-permute-done
  15.3 1.2 collective-permute-done.1
  16.5 0.1 concatenate.7
  16.6 0.1 slice_reduce_fusion
  16.7 0.1 and_reduce_fusion
  16.8 0.1 fusion.35
  16.8 34.8 %convert_reduce_fusion = f32[4126]{0:T(1024)S(1)} fusion(s32[4126]{0:T(1024)S(1)} %slice_reduce_fusion, s32[4096]{0:T(1024)S(1)} %broadcast_add_fusion), kind=kLoop, calls=%fused_computation.3 | loop fusion | flops 185896928 | bytes 49392 | tf_op jit(solution)/shard_map/reduce_sum | solution.py:62
  51.6 28.8 %scatter_custom_fusion.1 = f32[32768]{0:T(1024)S(1)} fusion(s32[4126]{0:T(1024)S(1)} %fusion.35, f32[4126]{0:T(1024)S(1)} %broadcast_select_fusion, f32[]{:T(128)} %constant.122.clone.1), kind=kCustom, calls=%fused_computation.41 | custom fusion | flops 4126 | bytes 131076 | tf_op jit(solution)/shard_map/scatter-add | solution.py:79
  80.4 0.6 convert_element_type.26
  81.1 0.0 all-reduce.7.cloned.1.call-update
  81.1 0.2 reduce-scatter.2.cloned.1.call-start
  81.3 35.3 %fusion.7 = f32[4126,128]{1,0:T(8,128)} fusion(s32[4096]{0:T(1024)S(1)} %broadcast_add_fusion, s32[4126]{0:T(1024)S(1)} %slice_reduce_fusion, pred[4126]{0:T(1024)(128)(4,1)S(1)} %and_reduce_fusion, pred[128,4096]{1,0:T(32,128)(4,1)S(1)} %iota_compare_fusion.5), kind=kOutput, calls=%fused_computation.12 | convolution fusion | flops 4462153728 | bytes 2673814 | tf_op jit(solution)/shard_map/dot_general | solution.py:59
  116.6 37.3 %scatter_custom_fusion = f32[32768,128]{1,0:T(8,128)} fusion(s32[4126]{0:T(1024)S(1)} %fusion.35, f32[4126,128]{1,0:T(8,128)} %fusion.7, f32[]{:T(128)} %constant.122.clone.1), kind=kCustom, calls=%fused_computation.10 | custom fusion | flops 528128 | bytes 16777728 | tf_op jit(solution)/shard_map/scatter-add | solution.py:69
  153.9 0.0 copy-start.2
  153.9 0.0 copy-start.1
  153.9 8.9 %convert_element_type.22 = bf16[32768,128]{1,0:T(8,128)(2,1)} convert(f32[32768,128]{1,0:T(8,128)} %scatter_custom_fusion) | non-fusion elementwise | flops 4194304 | bytes 25165824 | tf_op jit(solution)/shard_map/convert_element_type | solution.py:99
  162.8 0.0 reduce-scatter.2.cloned.1.call-update
  162.8 0.0 all-reduce.5.cloned.1.call-start
  162.9 0.0 copy-done.2
  162.9 0.6 dynamic-slice.6
  164.1 0.0 copy-done.1
  164.1 0.0 copy-done
  164.2 1.8 gather_fusion
  166.0 56.4 %all-reduce.7.cloned.1.call-done = bf16[32768]{0:T(1024)(128)(2,1)} async-done(((bf16[32768]{0:T(1024)(128)(2,1)}), bf16[32768]{0:T(1024)(128)(2,1)}) %all-reduce.7.cloned.1.call-update) | async-done | bytes 65552
  222.4 1.3 convert_reduce_fusion.2
  223.7 229.9 %reduce-scatter.2.cloned.1.call-done = bf16[1024,128]{1,0:T(8,128)(2,1)} async-done(((bf16[32768,128]{1,0:T(8,128)(2,1)}), bf16[1024,128]{1,0:T(8,128)(2,1)}) %reduce-scatter.2.cloned.1.call-update) | async-done | bytes 262160 | tf_op jit(solution)/shard_map/reduce_scatter | solution.py:96
  453.6 1.1 convert_reduce_fusion.1
  454.7 78.5 %all-reduce.1 = (f32[128]{0:T(128)S(1)}, f32[]{:T(128)}) all-reduce(f32[128]{0:T(128)S(1)} %convert_reduce_fusion.1, f32[]{:T(128)} %get-tuple-element.19), channel_id=1, replica_groups=mesh['stream'=32,'item'=8] {'stream','item'}, use_global_device_ids=true, to_apply=%region_8.9 | all-reduce | flops 129 | bytes 1032 | tf_op jit(solution)/shard_map/psum | solution.py:107
  533.9 3.0 fusion.14
  536.9 0.0 all-reduce.5.cloned.1.call-update
  536.9 237.6 %all-reduce.5.cloned.1.call-done = f32[128,256]{1,0:T(8,128)} async-done(((f32[128,256]{1,0:T(8,128)}), f32[128,256]{1,0:T(8,128)}) %all-reduce.5.cloned.1.call-update) | async-done | bytes 131088 | tf_op jit(solution)/shard_map/psum | solution.py:120
  774.5 1.3 dynamic-slice_multiply_fusion
  (5 shorter events, 0.0 us)
Async XLA Ops:
  6.5 157.6 %copy-start = (s32[15,32768]{1,0:T(8,128)S(1)}, s32[15,32768]{1,0:T(8,128)}, u32[]{:S(2)}) copy-start(s32[15,32768]{1,0:T(8,128)} %param.7) | copy-start | bytes 5898244
  6.5 215.9 %all-reduce.7.cloned.1.call-start = ((), (), s32[]{:S(2)}) async-start(), calls=%async_computation.3 | async-start | bytes 131072
  8.2 7.1 collective-permute-start
  12.2 4.3 collective-permute-start.1
  81.1 372.5 %reduce-scatter.2.cloned.1.call-start = ((), (), s32[]{:S(2)}) async-start(), calls=%async_computation.1 | async-start | bytes 8650752 | tf_op jit(solution)/shard_map/reduce_scatter | solution.py:96
  153.9 9.0 %copy-start.2 = (u32[256]{0:T(256)S(1)}, u32[256]{0:T(256)}, u32[]{:S(2)}) copy-start(u32[256]{0:T(256)} %constant.143) | copy-start | bytes 3076
  153.9 10.3 %copy-start.1 = (s32[270]{0:T(512)S(1)}, s32[270]{0:T(512)}, u32[]{:S(2)}) copy-start(s32[270]{0:T(512)} %constant.140) | copy-start | bytes 3244
  162.8 611.7 %all-reduce.5.cloned.1.call-start = ((), (), s32[]{:S(2)}) async-start(), calls=%async_computation.2 | async-start | bytes 262144 | tf_op jit(solution)/shard_map/psum | solution.py:120
Sparse Core Ops, SparseCore 0:
  81.2 141.1 all-reduce.6
  226.4 227.1 reduce-scatter.1
  537.0 237.4 all-reduce.4
where the time goes:
time: 783 us; the launch traced here: 782 us
  waiting for transfers between devices  525 us (67%)
  other arithmetic  118 us (15%)
  blocking collectives  78.5 us (10%)
  matrix products  38.3 us (5%)
  between operations  14.6 us (2%)
    psum x1, waiting for transfers between devices, local(): summed = lax.psum(partial_value, ('stream', 'item'))  238 us
    reduce_scatter x1, waiting for transfers between devices, local(): lax.psum_scatter(tile_block(pair_links, extended[0], band_start, owned_co...  230 us
    psum x1, blocking collectives, local(): lax.psum((jnp.sum(count_tile, axis=0), jnp.sum(col_margin)), ('stream', '...  78.5 us
    unnamed x4, waiting for transfers between devices  56.5 us
    scatter-add x1, other arithmetic, tile_block(): jax.ops.segment_sum(jnp.where(in_band[:, None], links_float, 0.0), jnp.wh...  37.3 us
    dot_general x1, matrix products, slab_pairs(): lax.dot_general(banded, row_hot, (((0,), (1,)), ((), ())), preferred_elem...  35.3 us
    reduce_sum x1, other arithmetic, slab_pairs(): weights = jnp.sum(banded, axis=0, dtype=jnp.float32)  34.8 us
    scatter-add x1, other arithmetic, band_counts(): jax.ops.segment_sum(jnp.where(in_band, weights, 0.0), jnp.where(in_band,...  28.8 us
  transfers between devices with their start and end apart: 5, of which 4 were waited for; matrix products, arithmetic and copies ran while one was open for 11% of the time, Pallas kernels for 0%

commit v1 on v0

v1 whole, which is shorter than its diff:
```python
import math

import jax
import jax.numpy as jnp
from jax import lax
from jax.experimental import pallas as pl
from jax.experimental.pallas import tpu as pltpu
from jax.sharding import PartitionSpec as P

SKETCH = 256
WINDOW = 15
ROWS = 128
ROWS_DEV = 4
LANES = 128
SLABS = 32
BANDS = 8
SLAB_ROWS = 32
HALF_ROWS = SLAB_ROWS // 2
PAYLOAD = 32
EVENT_ROWS = SLABS * SLAB_ROWS
OWNED = 1024
COLS = OWNED + ROWS
WORD_BITS = 18
WORDS = 15
SLOTS = 384
PAD = 8
MARGIN_ROW, TOTAL_ROW, BITS_ROW = 24, 25, 26
VMEM_BYTES = 48 << 20


def iota(shape, axis, dtype=jnp.int32):
    out = lax.broadcasted_iota(jnp.int32, shape, axis)
    return out if dtype == jnp.int32 else out.astype(dtype)


def nt_dot(left, right):
    return lax.dot_general(
        left, right, (((1,), (1,)), ((), ())), preferred_element_type=jnp.float32
    )


def hot(mask):
    return jnp.where(mask, 1.0, 0.0)


def pack_kernel(where, items_ref, sessions_ref, bits_ref, out_ref):
    _, band = where()
    half = lax.rem(band, 2)
    items, sessions = items_ref[...], sessions_ref[...]
    shape = items.shape
    row, lane = iota(shape, 0), iota(shape, 1)
    above = jnp.where(row == 0, -1, pltpu.roll(sessions, 1, 0))
    below = jnp.where(row == SLAB_ROWS - 1, -1, pltpu.roll(sessions, SLAB_ROWS - 1, 0))
    weights = jnp.zeros(shape, jnp.float32)
    for d in range(1, WINDOW + 1):
        earlier = pltpu.roll(jnp.where(lane >= LANES - d, above, sessions), d, 1)
        later = pltpu.roll(jnp.where(lane < d, below, sessions), LANES - d, 1)
        weights += hot(earlier == sessions) + hot(later == sessions)
    held = jnp.zeros((ROWS, LANES), jnp.float32)
    item_row = iota((ROWS, LANES), 0)
    for r in range(SLAB_ROWS):
        held += jnp.where(items[r : r + 1] == item_row, weights[r : r + 1], 0.0)
    margin = jnp.sum(held.T, axis=0, keepdims=True).astype(jnp.int32)
    total = jnp.sum(weights, axis=0, keepdims=True).astype(jnp.int32)
    own_items = jnp.where(half == 0, items[:HALF_ROWS], items[HALF_ROWS:])
    own_sessions = jnp.where(half == 0, sessions[:HALF_ROWS], sessions[HALF_ROWS:])
    pairs = own_sessions[:8] + own_sessions[8:] * 65536
    slab, _ = where()
    word = bits_ref[...]
    one = jnp.sum(
        jnp.where(iota(word.shape, 0) == jnp.minimum(slab, WORDS - 1), word, 0),
        axis=0,
        keepdims=True,
    )
    extra = jnp.concatenate([margin, total, one, jnp.zeros((5, LANES), jnp.int32)], axis=0)
    message = jnp.concatenate([own_items, pairs, extra], axis=0)
    for s in range(SLABS):
        out_ref[s] = message


def sketch_kernel(
    where, own_ref, other_ref, bits_hbm, out_ref,
    sess, codes, mask, table, counts, words, signs, sem,
):
    slab, band = where()
    half = lax.rem(band, 2)
    copy = pltpu.make_async_copy(
        bits_hbm.at[:, pl.ds(pl.multiple_of(slab * OWNED, OWNED), OWNED)],
        words,
        sem,
    )
    copy.start()
    lane_s = iota((SLAB_ROWS, LANES), 1)
    block_id = band * SLABS + slab
    pair_id = jnp.where(band < 2, 2 * slab + half, -1)

    edge = jnp.full((PAD, LANES), -(ROWS + 1.0), jnp.float32)
    codes[pl.ds(0, PAD), :] = edge
    codes[pl.ds(PAD + EVENT_ROWS, PAD), :] = edge
    sess[pl.ds(0, PAD), :] = jnp.full((PAD, LANES), -1, jnp.int32)

    def halves(s):
        mine, its = own_ref[s], other_ref[s]
        return jnp.where(half == 0, mine, its), jnp.where(half == 0, its, mine)

    def unpack(s, carry):
        first, second = halves(s)
        items = jnp.concatenate([first[:16], second[:16]], axis=0)
        a, b = first[16:24], second[16:24]
        sessions = jnp.concatenate([a & 65535, a >> 16, b & 65535, b >> 16], axis=0)
        base = pl.multiple_of(s * SLAB_ROWS, SLAB_ROWS)
        sess[pl.ds(PAD + base, SLAB_ROWS), :] = sessions
        above = sess[pl.ds(PAD - 1 + base, SLAB_ROWS), :]
        before = pltpu.roll(jnp.where(lane_s == LANES - 1, above, sessions), 1, 1)
        value = jnp.minimum(items, ROWS) + 1
        codes[pl.ds(PAD + base, SLAB_ROWS), :] = jnp.where(
            before != sessions, -value, value
        ).astype(jnp.float32)
        is_row = items < ROWS
        owned = jnp.where(is_row, items >> 1, items >> 10) == jnp.where(is_row, pair_id, block_id)
        ident = jnp.where(is_row, OWNED + items, items & (OWNED - 1))
        rows = pl.ds(base, SLAB_ROWS)
        mask[rows, :] = hot(owned).astype(jnp.bfloat16)
        table[rows, pl.ds(LANES, LANES)] = (ident & 255).astype(jnp.float32).astype(jnp.bfloat16)
        table[rows, pl.ds(2 * LANES, LANES)] = (ident >> 8).astype(jnp.float32).astype(jnp.bfloat16)
        return carry

    lax.fori_loop(0, SLABS, unpack, 0, unroll=4)
    for r in range(0, EVENT_ROWS, 128):
        rows = pl.ds(r, 128)
        table[rows, pl.ds(3 * LANES, LANES)] = codes[pl.ds(PAD - 1 + r, 128), :].astype(jnp.bfloat16)
        table[rows, pl.ds(4 * LANES, LANES)] = codes[pl.ds(PAD + r, 128), :].astype(jnp.bfloat16)
        table[rows, pl.ds(5 * LANES, LANES)] = codes[pl.ds(PAD + 1 + r, 128), :].astype(jnp.bfloat16)

    upto = hot(iota((LANES, LANES), 0) <= iota((LANES, LANES), 1)).astype(jnp.bfloat16)
    owned = mask[...]
    rank = jnp.dot(owned, upto, preferred_element_type=jnp.float32)
    table[:, pl.ds(0, LANES)] = (rank * owned.astype(jnp.float32)).astype(jnp.bfloat16)
    per_row = nt_dot(jnp.ones((8, LANES), jnp.bfloat16), owned)
    groups = EVENT_ROWS // LANES
    grouped = jnp.concatenate(
        [per_row[:1, g * LANES : (g + 1) * LANES] for g in range(groups)], axis=0
    )
    inside = jnp.dot(grouped.astype(jnp.bfloat16), upto, preferred_element_type=jnp.float32)
    ends, starts, base = [], [], jnp.zeros((1, 1), jnp.float32)
    for g in range(groups):
        ends.append(inside[g : g + 1] + base)
        starts.append(ends[g] - grouped[g : g + 1])
        base = base + inside[g : g + 1, LANES - 1 :]
    owned_events = jnp.max(base).astype(jnp.int32)

    counts[...] = jnp.zeros(counts.shape, jnp.float32)
    lane_f = iota((SLOTS, LANES), 1, jnp.float32)
    row32, col32 = iota((32, 32), 0), iota((32, 32), 1)
    ahead = (row32 > WINDOW) & (col32 > WINDOW) & (col32 <= row32)
    behind = (row32 < WINDOW) & (col32 > row32) & (col32 <= WINDOW)
    between = hot(ahead | behind).astype(jnp.bfloat16)
    place = iota((32, SLOTS), 0)
    in_window = (place != WINDOW) & (place <= 2 * WINDOW)
    row_ids = iota((ROWS, SLOTS), 0, jnp.float32)
    col_ids = iota((SLOTS, COLS), 1, jnp.float32)

    def chunk(step, carry):
        slot = (step * SLOTS + iota((SLOTS, LANES), 0)).astype(jnp.float32)
        picks, first = [], jnp.zeros((SLOTS, LANES), jnp.float32)
        for g in range(groups):
            here = (slot >= starts[g]) & (slot < ends[g])
            first += jnp.where(here, starts[g], 0.0)
            picks.append(hot(here).astype(jnp.bfloat16))
        pick = jnp.concatenate(picks, axis=1)
        got = jnp.dot(pick, table[...], preferred_element_type=jnp.float32)
        ordinal = slot[:, :1] + 1.0 - jnp.sum(first, axis=1, keepdims=True)
        chosen = got[:, :LANES] == ordinal
        ident = got[:, LANES : 2 * LANES] + 256.0 * got[:, 2 * LANES : 3 * LANES]
        column = jnp.sum(jnp.where(chosen, ident + 1.0, 0.0), axis=1, keepdims=True) - 1.0
        at_lane = jnp.sum(jnp.where(chosen, lane_f, 0.0), axis=1, keepdims=True)
        source = at_lane.astype(jnp.int32) + (iota((SLOTS, LANES), 1) - WINDOW)
        index = source & (LANES - 1)
        parts = [
            jnp.take_along_axis(got[:, k * LANES : (k + 1) * LANES], index, axis=1, mode="promise_in_bounds")
            for k in (3, 4, 5)
        ]
        window = jnp.where(source < 0, parts[0], jnp.where(source < LANES, parts[1], parts[2]))
        window = window.T[:32]
        breaks = hot(window < 0.0).astype(jnp.bfloat16)
        crossed = jnp.dot(between, breaks, preferred_element_type=jnp.float32)
        linked = (crossed == 0.0) & in_window
        near = jnp.where(linked, jnp.abs(window) - 1.0, 255.0)
        weight = jnp.sum(hot(linked), axis=0, keepdims=True)
        pairs = jnp.zeros((ROWS, SLOTS), jnp.float32)
        for d in range(2 * WINDOW + 1):
            if d != WINDOW:
                pairs += hot(near[d : d + 1] == row_ids)
        pairs = jnp.concatenate([pairs, jnp.broadcast_to(weight, (16, SLOTS))], axis=0)
        column_hot = hot(column == col_ids).astype(jnp.bfloat16)
        counts[...] += jnp.dot(
            pairs.astype(jnp.bfloat16), column_hot, preferred_element_type=jnp.float32
        )
        return carry

    lax.fori_loop(0, (owned_events + SLOTS - 1) // SLOTS, chunk, 0)

    def both(row_first, row_second):
        mine_f, its_f = own_ref[:, row_first, :], other_ref[:, row_first, :]
        mine_s, its_s = own_ref[:, row_second, :], other_ref[:, row_second, :]
        return jnp.where(half == 0, mine_f, its_f), jnp.where(half == 0, its_s, mine_s)

    start_items, end_items = both(0, 15)
    start_sess, end_sess = both(16, 23)
    start_sess, end_sess = start_sess & 65535, end_sess >> 16
    slab_row = iota((SLABS, LANES), 0)
    end_items = pltpu.roll(end_items, 1, 0)
    end_sess = jnp.where(slab_row == 0, -1, pltpu.roll(end_sess, 1, 0))
    cross = jnp.zeros((SLABS, LANES), jnp.float32)
    lane = iota((SLABS, LANES), 1)
    for d in range(1, WINDOW + 1):
        before = pltpu.roll(end_sess, d, 1)
        after = pltpu.roll(start_sess, LANES - d, 1)
        cross += hot((lane < d) & (before == start_sess))
        cross += hot((lane >= LANES - d) & (after == end_sess))
    cross_items = jnp.where(lane < LANES // 2, start_items, end_items)
    margins = jnp.sum(own_ref[:, MARGIN_ROW, :], axis=0, keepdims=True).astype(jnp.float32)
    item_row = iota((ROWS, LANES), 0)
    held = jnp.where(item_row == iota((ROWS, LANES), 1), margins, 0.0)
    for s in range(SLABS):
        held += jnp.where(cross_items[s : s + 1] == item_row, cross[s : s + 1], 0.0)
    row_margin = jnp.sum(held, axis=1, keepdims=True)
    totals = jnp.sum(own_ref[:, TOTAL_ROW, :], axis=0, keepdims=True).astype(jnp.float32)
    totals = totals + jnp.sum(cross, axis=0, keepdims=True)
    pair_total = jnp.sum(totals, axis=1, keepdims=True)

    count = counts[pl.ds(0, ROWS), :]
    col_margin = counts[pl.ds(ROWS, 1), :]
    log_ratio = (
        jnp.log(jnp.maximum(count, 1.0))
        + jnp.log(pair_total)
        - jnp.log(jnp.maximum(row_margin, 1.0))
        - jnp.log(jnp.maximum(col_margin, 1.0))
    )
    positive = jnp.where(count > 0, jnp.maximum(log_ratio, 0.0), 0.0)
    high = positive.astype(jnp.bfloat16)
    rest = positive - high.astype(jnp.float32)
    mid = rest.astype(jnp.bfloat16)
    low = (rest - mid.astype(jnp.float32)).astype(jnp.bfloat16)
    parts = jnp.concatenate([high, mid, low], axis=0)

    copy.wait()
    row_words = jnp.where(half == 0, own_ref[:WORDS, BITS_ROW, :], other_ref[:WORDS, BITS_ROW, :])
    held_words = jnp.concatenate([words[...], row_words], axis=1)
    held_words = jnp.concatenate([held_words, jnp.zeros((1, COLS), jnp.int32)], axis=0)
    for b in range(WORD_BITS):
        signs[pl.ds(b * 16, 16), :] = jnp.where((held_words >> b) & 1 == 1, 1.0, -1.0).astype(jnp.bfloat16)
    by_bit = nt_dot(parts, signs[...])
    by_bit = by_bit[:ROWS] + (by_bit[ROWS : 2 * ROWS] + by_bit[2 * ROWS :])
    have = iota((16 * WORD_BITS, SKETCH), 0)
    want = iota((16 * WORD_BITS, SKETCH), 1)
    order = hot((have & 15) * WORD_BITS + (have >> 4) == want).astype(jnp.bfloat16)
    high = by_bit.astype(jnp.bfloat16)
    rest = by_bit - high.astype(jnp.float32)
    mid = rest.astype(jnp.bfloat16)
    low = (rest - mid.astype(jnp.float32)).astype(jnp.bfloat16)
    moved = jnp.dot(
        jnp.concatenate([high, mid, low], axis=0), order, preferred_element_type=jnp.float32
    )
    result = moved[:ROWS] + (moved[ROWS : 2 * ROWS] + moved[2 * ROWS :])
    for s in range(SLABS):
        out_ref[s] = result[s * ROWS_DEV : (s + 1) * ROWS_DEV]


def pack(where, items, sessions, bits, interpret=False):
    return pl.pallas_call(
        lambda *refs: pack_kernel(where, *refs),
        out_shape=jax.ShapeDtypeStruct((SLABS, PAYLOAD, LANES), jnp.int32),
        grid=(1,),
        in_specs=[
            pl.BlockSpec((SLAB_ROWS, LANES), lambda i: (0, 0)),
            pl.BlockSpec((SLAB_ROWS, LANES), lambda i: (0, 0)),
            pl.BlockSpec((WORDS, LANES), lambda i: (0, 0)),
        ],
        out_specs=pl.BlockSpec((SLABS, PAYLOAD, LANES), lambda i: (0, 0, 0)),
        compiler_params=pltpu.CompilerParams(vmem_limit_bytes=VMEM_BYTES),
        interpret=interpret,
        name="pack_events",
    )(items, sessions, bits)


def sketch_part(where, own, other, bits, interpret=False):
    return pl.pallas_call(
        lambda *refs: sketch_kernel(where, *refs),
        out_shape=jax.ShapeDtypeStruct((SLABS, ROWS_DEV, SKETCH), jnp.float32),
        in_specs=[
            pl.BlockSpec(memory_space=pltpu.VMEM),
            pl.BlockSpec(memory_space=pltpu.VMEM),
            pl.BlockSpec(memory_space=pl.ANY),
        ],
        out_specs=pl.BlockSpec(memory_space=pltpu.VMEM),
        scratch_shapes=[
            pltpu.VMEM((PAD + EVENT_ROWS, LANES), jnp.int32),
            pltpu.VMEM((2 * PAD + EVENT_ROWS, LANES), jnp.float32),
            pltpu.VMEM((EVENT_ROWS, LANES), jnp.bfloat16),
            pltpu.VMEM((EVENT_ROWS, 6 * LANES), jnp.bfloat16),
            pltpu.VMEM((ROWS + 16, COLS), jnp.float32),
            pltpu.VMEM((WORDS, OWNED), jnp.int32),
            pltpu.VMEM((16 * WORD_BITS, COLS), jnp.bfloat16),
            pltpu.SemaphoreType.DMA,
        ],
        compiler_params=pltpu.CompilerParams(vmem_limit_bytes=VMEM_BYTES),
        interpret=interpret,
        name="sketch_part",
    )(own, other, bits)


def local(event_items, event_sessions, sketch_bits):
    def where():
        return lax.axis_index("stream"), lax.axis_index("item")

    message = pack(
        where,
        event_items.reshape(SLAB_ROWS, LANES),
        event_sessions.reshape(SLAB_ROWS, LANES),
        sketch_bits,
    )
    own = lax.all_to_all(message, "stream", 0, 0, tiled=True)
    other = lax.ppermute(own, "item", [(i, i ^ 1) for i in range(BANDS)])
    part = sketch_part(where, own, other, sketch_bits)
    rows = jnp.sum(lax.all_to_all(part, "stream", 0, 0, tiled=True), axis=0)
    spread = jnp.broadcast_to(rows[None], (BANDS,) + rows.shape)
    summed = jnp.sum(lax.all_to_all(spread, "item", 0, 0, tiled=True), axis=0)
    return summed / math.sqrt(EVENT_ROWS * LANES)


def solution(mesh):
    placed = (P("stream"), P("stream"), P(None, "item"))
    return jax.shard_map(
        local, mesh=mesh, in_specs=placed, out_specs=P("stream", None), check_vma=False
    )
```

time: 783 us -> 72.4 us (0.09)
  waiting for transfers between devices: 525 us -> 1.54 us
  other arithmetic: 118 us -> 0.66 us
  matrix products: 38.3 us -> 0 us
  blocking collectives: 78.5 us -> 51 us
  between operations: 14.6 us -> 0.03 us
  Pallas kernels: 0 us -> 13.4 us
    psum x1 -> x0, waiting for transfers between devices: 238 us -> none  [local(): summed = lax.psum(partial_value, ('stream', 'item'))]
    reduce_scatter x1 -> x0, waiting for transfers between devices: 230 us -> none  [local(): lax.psum_scatter(tile_block(pair_links, extended[0], band_start, owned_co...]
    psum x1 -> x0, blocking collectives: 78.5 us -> none  [local(): lax.psum((jnp.sum(count_tile, axis=0), jnp.sum(col_margin)), ('stream', '...]
    scatter-add x2 -> x0, other arithmetic: 66 us -> none  [the longest x1 37.3 us: tile_block(): jax.ops.segment_sum(jnp.where(in_band[:, None], links_float, 0.0), jnp.wh...]
    unnamed x4 -> x0, waiting for transfers between devices: 56.5 us -> none
    all_to_all x0 -> x3, blocking collectives: none -> 51 us  [the longest x1 28.2 us: local(): own = lax.all_to_all(message, 'stream', 0, 0, tiled=True)]
    dot_general x2 -> x0, matrix products: 38.3 us -> none  [the longest x1 35.3 us: slab_pairs(): lax.dot_general(banded, row_hot, (((0,), (1,)), ((), ())), preferred_elem...]
    reduce_sum x3 -> x2, other arithmetic: 37.2 us -> 0.06 us  [the longest x1 0.04 us: local(): rows = jnp.sum(lax.all_to_all(part, 'stream', 0, 0, tiled=True), axis=0)]
  transfers between devices with their start and end apart: 5 -> 1, of which waited for: 4 -> 1; matrix products, arithmetic and copies ran while one was open for 11% -> 0% of each run, Pallas kernels for 0% -> 0%
where the time goes in v1:
time: 72.4 us; the launch traced here: 72.1 us
  blocking collectives  51 us (70%)
  Pallas kernels  13.4 us (19%)
  local copies, waits for them, and re-layouts  3.04 us (4%)
  starting transfers between devices  2.39 us (3%)
  waiting for transfers between devices  1.54 us (2%)
    all_to_all x1, blocking collectives, local(): own = lax.all_to_all(message, 'stream', 0, 0, tiled=True)  28.2 us
    all_to_all x1, blocking collectives, local(): rows = jnp.sum(lax.all_to_all(part, 'stream', 0, 0, tiled=True), axis=0)  13.6 us
    pallas_call x1, Pallas kernels, sketch_part(): pl.pallas_call(lambda *refs: sketch_kernel(where, *refs), out_shape=jax.S...  12.9 us
    all_to_all x1, blocking collectives, local(): summed = jnp.sum(lax.all_to_all(spread, 'item', 0, 0, tiled=True), axis=0)  9.17 us
    unnamed x8, local copies, waits for them, and re-layouts  3.03 us
    ppermute x1, starting transfers between devices, local(): other = lax.ppermute(own, 'item', [(i, i ^ 1) for i in range(BANDS)])  2.39 us
    ppermute x1, waiting for transfers between devices, local(): other = lax.ppermute(own, 'item', [(i, i ^ 1) for i in range(BANDS)])  1.54 us
  transfers between devices with their start and end apart: 1, of which 1 were waited for; matrix products, arithmetic and copies ran while one was open for 0% of the time, Pallas kernels for 0%

profile of v1, /device:TPU:1, one launch (start us, length us, event | category | flops | bytes accessed | tf_op | source)
XLA Modules:
  0.0 72.1 jit_solution(3665885007775585409)
XLA Ops:
  0.0 0.0 copy-start
  0.0 1.6 %copy-done = s32[15,32768]{1,0:T(8,128)S(1)} copy-done((s32[15,32768]{1,0:T(8,128)S(1)}, s32[15,32768]{1,0:T(8,128)}, u32[]{:S(2)}) %copy-start) | copy-done | bytes 1966104
  1.6 0.0 copy-start.2
  1.6 0.7 copy-done.2
  2.3 0.0 copy-start.3
  2.3 0.7 copy-done.3
  3.0 0.0 copy-start.1
  3.0 0.5 pack_events.1
  3.6 28.2 %all_to_all.15.refs_0_ = s32[32,32,128]{2,1,0:T(8,128)S(1)} all-to-all(s32[32,32,128]{2,1,0:T(8,128)S(1)} %pack_events.1), channel_id=1, replica_groups=mesh['stream'=32,'item'=8] {'stream'}, dimensions={0} | all-to-all | bytes 1048576 | tf_op jit(solution)/shard_map/all_to_all | solution.py:323
  31.8 2.4 %collective-permute-start = (s32[32,32,128]{2,1,0:T(8,128)S(1)}, s32[32,32,128]{2,1,0:T(8,128)S(1)}, u32[]{:S(2)}, u32[]{:S(2)}) collective-permute-start(s32[32,32,128]{2,1,0:T(8,128)S(1)} %all_to_all.15.refs_0_), channel_id=1, source_target_pairs={{0,1},{1,0},{2,3},{3,2},{4,5},{5,4},{6,7},{7,6},{8,9},{9,8},{10,11... | collective-permute-start | bytes 1572872 | tf_op jit(solution)/shard_map/ppermute | solution.py:324
  34.2 1.5 %collective-permute-done.refs_1_ = s32[32,32,128]{2,1,0:T(8,128)S(1)} collective-permute-done((s32[32,32,128]{2,1,0:T(8,128)S(1)}, s32[32,32,128]{2,1,0:T(8,128)S(1)}, u32[]{:S(2)}, u32[]{:S(2)}) %collective-permute-start) | collective-permute-done | bytes 524320 | tf_op jit(solution)/shard_map/ppermute | solution.py:324
  35.7 0.0 copy-done.1
  35.7 12.9 %sketch_part.1 = f32[32,4,256]{2,1,0:T(4,128)S(1)} custom-call(s32[32,32,128]{2,1,0:T(8,128)S(1)} %all_to_all.15.refs_0_, s32[32,32,128]{2,1,0:T(8,128)S(1)} %collective-permute-done.refs_1_, s32[15,32768]{1,0:T(8,128)S(1)} %copy-done.1), custom_call_target="tpu_custom_call" | custom-call | tf_op jit(solution)/shard_map/sketch_part/pallas_call | solution.py:288
  48.7 13.6 %all_to_all.16 = f32[32,4,256]{2,1,0:T(4,128)S(1)} all-to-all(f32[32,4,256]{2,1,0:T(4,128)S(1)} %sketch_part.1), channel_id=1, replica_groups=mesh['stream'=32,'item'=8] {'stream'}, dimensions={0} | all-to-all | bytes 262144 | tf_op jit(solution)/shard_map/all_to_all | solution.py:326
  62.3 9.2 %all_to_all.17 = f32[8,4,256]{2,1,0:T(4,128)S(1)} all-to-all(f32[8,4,256]{2,1,0:T(4,128)S(1)} %broadcast_in_dim.2), channel_id=1, replica_groups=mesh['stream'=32,'item'=8] {'item'}, dimensions={0} | all-to-all | bytes 65536 | tf_op jit(solution)/shard_map/all_to_all | solution.py:328
  71.5 0.6 broadcast_multiply_fusion
  (3 shorter events, 0.1 us)
Async XLA Ops:
  0.0 1.6 %copy-start = (s32[15,32768]{1,0:T(8,128)S(1)}, s32[15,32768]{1,0:T(8,128)}, u32[]{:S(2)}) copy-start(s32[15,32768]{1,0:T(8,128)} %refs_2_.3) | copy-start | bytes 5898244
  1.6 0.7 copy-start.2
  2.3 0.7 copy-start.3
  3.0 32.7 %copy-start.1 = (s32[15,32768]{1,0:T(8,128)S(1)}, s32[15,32768]{1,0:T(8,128)}, u32[]{:S(2)}) copy-start(s32[15,32768]{1,0:T(8,128)} %refs_2_.3) | copy-start | bytes 5898244
  31.8 3.9 %collective-permute-start = (s32[32,32,128]{2,1,0:T(8,128)S(1)}, s32[32,32,128]{2,1,0:T(8,128)S(1)}, u32[]{:S(2)}, u32[]{:S(2)}) collective-permute-start(s32[32,32,128]{2,1,0:T(8,128)S(1)} %all_to_all.15.refs_0_), channel_id=1, source_target_pairs={{0,1},{1,0},{2,3},{3,2},{4,5},{5,4},{6,7},{7,6},{8,9},{9,8},{10,11... | collective-permute-start | bytes 1572872 | tf_op jit(solution)/shard_map/ppermute | solution.py:324

commit v2 on v1

--- a/solution.py
+++ b/solution.py
@@ -25,6 +25,9 @@
 SLOTS = 384
 PAD = 8
 MARGIN_ROW, TOTAL_ROW, BITS_ROW = 24, 25, 26
+QUOTA = 32
+MESSAGE = 16
+NONE = 255.0
 VMEM_BYTES = 48 << 20
 
 
@@ -43,7 +46,44 @@
     return jnp.where(mask, 1.0, 0.0)
 
 
-def pack_kernel(where, items_ref, sessions_ref, bits_ref, out_ref):
+def ppmi(count, row_margin, col_margin, pair_total):
+    log_ratio = (
+        jnp.log(jnp.maximum(count, 1.0))
+        + jnp.log(pair_total)
+        - jnp.log(jnp.maximum(row_margin, 1.0))
+        - jnp.log(jnp.maximum(col_margin, 1.0))
+    )
+    return jnp.where(count > 0, jnp.maximum(log_ratio, 0.0), 0.0)
+
+
+def split(values):
+    high = values.astype(jnp.bfloat16)
+    rest = values - high.astype(jnp.float32)
+    mid = rest.astype(jnp.bfloat16)
+    low = (rest - mid.astype(jnp.float32)).astype(jnp.bfloat16)
+    return jnp.concatenate([high, mid, low], axis=0)
+
+
+def joined(parts):
+    third = parts.shape[0] // 3
+    return parts[:third] + (parts[third : 2 * third] + parts[2 * third :])
+
+
+def fill_signs(held_words, signs):
+    held_words = jnp.concatenate([held_words, jnp.zeros((1, COLS), jnp.int32)], axis=0)
+    for b in range(WORD_BITS):
+        signs[pl.ds(b * 16, 16), :] = jnp.where((held_words >> b) & 1 == 1, 1.0, -1.0).astype(jnp.bfloat16)
+
+
+def project(positive, signs):
+    by_bit = joined(nt_dot(split(positive), signs[...]))
+    have = iota((16 * WORD_BITS, SKETCH), 0)
+    want = iota((16 * WORD_BITS, SKETCH), 1)
+    order = hot((have & 15) * WORD_BITS + (have >> 4) == want).astype(jnp.bfloat16)
+    return joined(jnp.dot(split(by_bit), order, preferred_element_type=jnp.float32))
+
+
+def all_events_kernel(where, items_ref, sessions_ref, bits_ref, out_ref):
     _, band = where()
     half = lax.rem(band, 2)
     items, sessions = items_ref[...], sessions_ref[...]
@@ -78,7 +118,7 @@
         out_ref[s] = message
 
 
-def sketch_kernel(
+def from_all_kernel(
     where, own_ref, other_ref, bits_hbm, out_ref,
     sess, codes, mask, table, counts, words, signs, sem,
 ):
@@ -229,47 +269,20 @@
     totals = totals + jnp.sum(cross, axis=0, keepdims=True)
     pair_total = jnp.sum(totals, axis=1, keepdims=True)
 
-    count = counts[pl.ds(0, ROWS), :]
-    col_margin = counts[pl.ds(ROWS, 1), :]
-    log_ratio = (
-        jnp.log(jnp.maximum(count, 1.0))
-        + jnp.log(pair_total)
-        - jnp.log(jnp.maximum(row_margin, 1.0))
-        - jnp.log(jnp.maximum(col_margin, 1.0))
-    )
-    positive = jnp.where(count > 0, jnp.maximum(log_ratio, 0.0), 0.0)
-    high = positive.astype(jnp.bfloat16)
-    rest = positive - high.astype(jnp.float32)
-    mid = rest.astype(jnp.bfloat16)
-    low = (rest - mid.astype(jnp.float32)).astype(jnp.bfloat16)
-    parts = jnp.concatenate([high, mid, low], axis=0)
-
+    positive = ppmi(
+        counts[pl.ds(0, ROWS), :], row_margin, counts[pl.ds(ROWS, 1), :], pair_total
+    )
     copy.wait()
     row_words = jnp.where(half == 0, own_ref[:WORDS, BITS_ROW, :], other_ref[:WORDS, BITS_ROW, :])
-    held_words = jnp.concatenate([words[...], row_words], axis=1)
-    held_words = jnp.concatenate([held_words, jnp.zeros((1, COLS), jnp.int32)], axis=0)
-    for b in range(WORD_BITS):
-        signs[pl.ds(b * 16, 16), :] = jnp.where((held_words >> b) & 1 == 1, 1.0, -1.0).astype(jnp.bfloat16)
-    by_bit = nt_dot(parts, signs[...])
-    by_bit = by_bit[:ROWS] + (by_bit[ROWS : 2 * ROWS] + by_bit[2 * ROWS :])
-    have = iota((16 * WORD_BITS, SKETCH), 0)
-    want = iota((16 * WORD_BITS, SKETCH), 1)
-    order = hot((have & 15) * WORD_BITS + (have >> 4) == want).astype(jnp.bfloat16)
-    high = by_bit.astype(jnp.bfloat16)
-    rest = by_bit - high.astype(jnp.float32)
-    mid = rest.astype(jnp.bfloat16)
-    low = (rest - mid.astype(jnp.float32)).astype(jnp.bfloat16)
-    moved = jnp.dot(
-        jnp.concatenate([high, mid, low], axis=0), order, preferred_element_type=jnp.float32
-    )
-    result = moved[:ROWS] + (moved[ROWS : 2 * ROWS] + moved[2 * ROWS :])
+    fill_signs(jnp.concatenate([words[...], row_words], axis=1), signs)
+    result = project(positive, signs)
     for s in range(SLABS):
         out_ref[s] = result[s * ROWS_DEV : (s + 1) * ROWS_DEV]
 
 
-def pack(where, items, sessions, bits, interpret=False):
+def all_events(where, items, sessions, bits, interpret=False):
     return pl.pallas_call(
-        lambda *refs: pack_kernel(where, *refs),
+        lambda *refs: all_events_kernel(where, *refs),
         out_shape=jax.ShapeDtypeStruct((SLABS, PAYLOAD, LANES), jnp.int32),
         grid=(1,),
         in_specs=[
@@ -280,13 +293,13 @@
         out_specs=pl.BlockSpec((SLABS, PAYLOAD, LANES), lambda i: (0, 0, 0)),
         compiler_params=pltpu.CompilerParams(vmem_limit_bytes=VMEM_BYTES),
         interpret=interpret,
-        name="pack_events",
+        name="all_events",
     )(items, sessions, bits)
 
 
-def sketch_part(where, own, other, bits, interpret=False):
+def from_all(where, own, other, bits, interpret=False):
     return pl.pallas_call(
-        lambda *refs: sketch_kernel(where, *refs),
+        lambda *refs: from_all_kernel(where, *refs),
         out_shape=jax.ShapeDtypeStruct((SLABS, ROWS_DEV, SKETCH), jnp.float32),
         in_specs=[
             pl.BlockSpec(memory_space=pltpu.VMEM),
@@ -306,29 +319,347 @@
         ],
         compiler_params=pltpu.CompilerParams(vmem_limit_bytes=VMEM_BYTES),
         interpret=interpret,
+        name="from_all",
+    )(own, other, bits)
+
+
+def route_kernel(where, items_hbm, sessions_hbm, out_ref, items_v, sessions_v, codes, table, near_rows, one_hots, pair_rows, sems):
+    slab, band = where()
+    get_items = pltpu.make_async_copy(items_hbm, items_v, sems.at[0])
+    get_sessions = pltpu.make_async_copy(sessions_hbm, sessions_v, sems.at[1])
+    get_items.start()
+    get_sessions.start()
+    get_items.wait()
+    get_sessions.wait()
+    items, sessions = items_v[...], sessions_v[...]
+    shape = items.shape
+    row, lane = iota(shape, 0), iota(shape, 1)
+    above = jnp.where(row == 0, -1, pltpu.roll(sessions, 1, 0))
+    below = jnp.where(row == SLAB_ROWS - 1, -1, pltpu.roll(sessions, SLAB_ROWS - 1, 0))
+    earlier_links = jnp.zeros(shape, jnp.float32)
+    later_links = jnp.zeros(shape, jnp.float32)
+    for d in range(1, WINDOW + 1):
+        earlier = pltpu.roll(jnp.where(lane >= LANES - d, above, sessions), d, 1)
+        later = pltpu.roll(jnp.where(lane < d, below, sessions), LANES - d, 1)
+        earlier_links += hot(earlier == sessions)
+        later_links += hot(later == sessions)
+    weights = earlier_links + later_links
+
+    held = jnp.zeros((ROWS, LANES), jnp.float32)
+    item_row = iota((ROWS, LANES), 0)
+    for r in range(SLAB_ROWS):
+        same = items[r : r + 1] == item_row
+        held += jnp.where(same, weights[r : r + 1], 0.0)
+        one_hots[:, pl.ds(r * LANES, LANES)] = hot(same).astype(jnp.bfloat16)
+    margin = jnp.sum(held.T, axis=0, keepdims=True)
+    total = jnp.sum(weights, axis=0, keepdims=True)
+    first_link = iota(shape, 1, jnp.float32) - earlier_links
+    place = iota((2 * LANES, LANES), 0, jnp.float32) - LANES
+    self_place = iota((2 * LANES, LANES), 1, jnp.float32)
+    sooner = place < self_place
+    for r in range(SLAB_ROWS):
+        links = hot(sooner & (place >= first_link[r : r + 1])).astype(jnp.bfloat16)
+        if r == 0:
+            pairs = jnp.dot(one_hots[:, pl.ds(0, LANES)], links[LANES:], preferred_element_type=jnp.float32)
+        else:
+            pairs = jnp.dot(
+                one_hots[:, pl.ds((r - 1) * LANES, 2 * LANES)], links, preferred_element_type=jnp.float32
+            )
+        pair_rows[:, pl.ds(r * LANES, LANES)] = pairs.astype(jnp.bfloat16)
+    ordered = nt_dot(pair_rows[...], one_hots[...])
+    row_pairs = ordered + ordered.T
+
+    before = pltpu.roll(jnp.where(lane == LANES - 1, above, sessions), 1, 1)
+    value = jnp.minimum(items, ROWS) + 1
+    edge = jnp.full((PAD, LANES), -(ROWS + 1.0), jnp.float32)
+    codes[pl.ds(0, PAD), :] = edge
+    codes[pl.ds(PAD + SLAB_ROWS, PAD), :] = edge
+    codes[pl.ds(PAD, SLAB_ROWS), :] = jnp.where(before != sessions, -value, value).astype(jnp.float32)
+    inside = items - band * (SLABS * OWNED)
+    wide = (items >= ROWS) & (inside >= 0) & (inside < SLABS * OWNED)
+    inside = jnp.where(wide, inside, 0)
+    owner = jnp.where(wide, inside >> 10, -1)
+    owner_row = iota((SLABS, LANES), 0)
+    marks = [hot(owner[r : r + 1] == owner_row) for r in range(SLAB_ROWS)]
+    upto = hot(iota((LANES, LANES), 0) <= iota((LANES, LANES), 1)).astype(jnp.bfloat16)
+    ranks = jnp.dot(
+        jnp.concatenate(marks, axis=0).astype(jnp.bfloat16), upto, preferred_element_type=jnp.float32
+    )
+    ranks = [ranks[r * SLABS : (r + 1) * SLABS] for r in range(SLAB_ROWS)]
+    per_row = jnp.zeros((SLABS, LANES), jnp.float32)
+    for r in range(SLAB_ROWS):
+        per_row = jnp.where(lane == r, ranks[r][:, LANES - 1 :], per_row)
+    ends = jnp.dot(per_row.astype(jnp.bfloat16), upto, preferred_element_type=jnp.float32)
+    starts = ends - per_row
+    most = jnp.max(ends[:, LANES - 1 :], axis=0, keepdims=True)
+    orders = [
+        jnp.sum(marks[r] * (ranks[r] + starts[:, r : r + 1]), axis=0, keepdims=True)
+        for r in range(SLAB_ROWS)
+    ]
+    table[pl.ds(SLAB_ROWS, LANES - SLAB_ROWS), :] = jnp.zeros((LANES - SLAB_ROWS, 6 * LANES), jnp.bfloat16)
+    fields = [
+        jnp.minimum(jnp.concatenate(orders, axis=0), 255.0),
+        (inside & 255).astype(jnp.float32),
+        (inside >> 8).astype(jnp.float32),
+        codes[pl.ds(PAD - 1, SLAB_ROWS), :],
+        codes[pl.ds(PAD, SLAB_ROWS), :],
+        codes[pl.ds(PAD + 1, SLAB_ROWS), :],
+    ]
+    for k, field in enumerate(fields):
+        table[pl.ds(0, SLAB_ROWS), pl.ds(k * LANES, LANES)] = field.astype(jnp.bfloat16)
+    slot = iota((QUOTA, LANES), 0, jnp.float32)
+    picks = [
+        hot((slot >= starts[s : s + 1]) & (slot < ends[s : s + 1])).astype(jnp.bfloat16)
+        for s in range(SLABS)
+    ]
+    got = jnp.dot(jnp.concatenate(picks, axis=0), table[...], preferred_element_type=jnp.float32)
+    big = (SLABS * QUOTA, LANES)
+    number, lanes = iota(big, 0), iota(big, 1)
+    target = (number >> 5).astype(jnp.float32) * 4.0
+    high = got[:, 2 * LANES : 3 * LANES] - target
+    ordinal = ((number & (QUOTA - 1)) + 1).astype(jnp.float32)
+    chosen = (got[:, :LANES] == ordinal) & (high >= 0.0) & (high < 4.0)
+    ident = got[:, LANES : 2 * LANES] + 256.0 * high
+    column = jnp.sum(jnp.where(chosen, ident + 1.0, 0.0), axis=1, keepdims=True) - 1.0
+    at_lane = jnp.sum(jnp.where(chosen, lanes.astype(jnp.float32), 0.0), axis=1, keepdims=True)
+    source = at_lane.astype(jnp.int32) + (lanes - WINDOW)
+    index = source & (LANES - 1)
+    parts = [
+        jnp.take_along_axis(got[:, k * LANES : (k + 1) * LANES], index, axis=1, mode="promise_in_bounds")
+        for k in (3, 4, 5)
+    ]
+    window = jnp.where(source < 0, parts[0], jnp.where(source < LANES, parts[1], parts[2]))
+    from_lane, to_lane = iota((LANES, LANES), 0), iota((LANES, LANES), 1)
+    ahead = (to_lane > WINDOW) & (from_lane > WINDOW) & (from_lane <= to_lane)
+    behind = (to_lane < WINDOW) & (from_lane > to_lane) & (from_lane <= WINDOW)
+    between = hot(ahead | behind).astype(jnp.bfloat16)
+    crossed = jnp.dot(
+        hot(window < 0.0).astype(jnp.bfloat16), between, preferred_element_type=jnp.float32
+    )
+    linked = (crossed == 0.0) & (lanes <= 2 * WINDOW)
+    near = jnp.where(linked, jnp.abs(window) - 1.0, NONE)
+    near_rows[...] = jnp.where(lanes == WINDOW, column, near)
+
+    ends_lane = iota((1, LANES), 1)
+    spare = jnp.where(most > QUOTA, 1.0, 0.0)
+    edge_items = jnp.where(ends_lane < LANES // 2, items[:1], items[SLAB_ROWS - 1 :]).astype(jnp.float32)
+    edge_items = jnp.where(ends_lane == LANES // 2, spare, edge_items)
+    edge_sessions = jnp.where(
+        ends_lane < LANES // 2, sessions[:1], sessions[SLAB_ROWS - 1 :]
+    ).astype(jnp.float32)
+    common = jnp.concatenate([margin, total, edge_items, edge_sessions], axis=0)
+    quarter = iota((8, LANES), 1) >> 5
+    for s in range(SLABS):
+        rows = near_rows[pl.ds(s * QUOTA, 8), :]
+        for g in range(1, QUOTA // 8):
+            part = pltpu.roll(near_rows[pl.ds(s * QUOTA + 8 * g, 8), :], 32 * g, 1)
+            rows = jnp.where(quarter == g, part, rows)
+        out_ref[s, pl.ds(0, 8), :] = rows
+        out_ref[s, pl.ds(8, 8), :] = jnp.concatenate(
+            [row_pairs[s * ROWS_DEV : (s + 1) * ROWS_DEV], common], axis=0
+        )
+
+
+def count_pairs(near, skip):
+    slots = near.shape[1]
+    row_ids = iota((ROWS, slots), 0, jnp.float32)
+    pairs = jnp.zeros((ROWS, slots), jnp.float32)
+    for d in range(near.shape[0]):
+        if d not in skip:
+            pairs += hot(near[d : d + 1] == row_ids)
+    place = iota(near.shape, 0)
+    real = near < NONE
+    for d in skip:
+        real = real & (place != d)
+    weight = jnp.sum(hot(real), axis=0, keepdims=True)
+    return jnp.concatenate([pairs, jnp.broadcast_to(weight, (16, slots))], axis=0).astype(jnp.bfloat16)
+
+
+def sketch_kernel(where, got_ref, row_bits_ref, bits_hbm, out_ref, counts, table, words, signs, sem):
+    slab, band = where()
+    copy = pltpu.make_async_copy(
+        bits_hbm.at[:, pl.ds(pl.multiple_of(slab * OWNED, OWNED), OWNED)], words, sem
+    )
+    copy.start()
+
+    windows = got_ref[:, :8, :].reshape(SLABS * 8, LANES).T
+    blocks, idents = [], []
+    for g in range(QUOTA // 8):
+        near = windows[32 * g : 32 * g + 32]
+        idents.append(near[WINDOW : WINDOW + 1])
+        blocks.append(count_pairs(near, (WINDOW, 31)))
+    ident = jnp.concatenate(idents, axis=1)
+    pairs = jnp.concatenate(blocks, axis=1)
+    column_hot = hot(ident == iota((OWNED, ident.shape[1]), 0, jnp.float32)).astype(jnp.bfloat16)
+    counts[:, pl.ds(0, OWNED)] = nt_dot(pairs, column_hot)
+
+    edge_items, edge_sessions = got_ref[:, 14, :], got_ref[:, 15, :]
+    overflow = jnp.max(edge_items[:, LANES // 2 : LANES // 2 + 1], axis=0, keepdims=True)
+    slab_row, lane = iota((SLABS, LANES), 0), iota((SLABS, LANES), 1)
+    end_items = pltpu.roll(edge_items, 1, 0)
+    end_sess = jnp.where(slab_row == 0, -1.0, pltpu.roll(edge_sessions, 1, 0))
+    cross = jnp.zeros((SLABS, LANES), jnp.float32)
+    for d in range(1, WINDOW + 1):
+        before = pltpu.roll(end_sess, d, 1)
+        after = pltpu.roll(edge_sessions, LANES - d, 1)
+        cross += hot((lane < d) & (before == edge_sessions))
+        cross += hot((lane >= LANES - d) & (after == end_sess))
+    items = jnp.where(lane < LANES // 2, edge_items, end_items)
+    over = jnp.where(
+        lane < LANES // 2,
+        hot((edge_sessions == end_sess[:, LANES - 1 :]) & (lane < WINDOW)),
+        hot((end_sess == edge_sessions[:, :1]) & (lane >= LANES - WINDOW)),
+    )
+    partner = jnp.where(over > 0.0, jnp.minimum(items, float(ROWS)), NONE)
+    whole = items.astype(jnp.int32)
+    is_row = whole < ROWS
+    row_owner = jnp.where(band == 0, slab, -1)
+    owned = jnp.where(is_row, whole >> 2, whole >> 10) == jnp.where(is_row, row_owner, band * SLABS + slab)
+    owned = hot(owned & (cross > 0.0))
+    local_id = jnp.where(is_row, OWNED + whole, whole & (OWNED - 1))
+    upto = hot(iota((LANES, LANES), 0) <= iota((LANES, LANES), 1)).astype(jnp.bfloat16)
+    blank = jnp.zeros((LANES - SLABS, LANES), jnp.float32)
+    marks = jnp.concatenate([owned, blank], axis=0).astype(jnp.bfloat16)
+    rank = jnp.dot(marks, upto, preferred_element_type=jnp.float32)
+    per_row = nt_dot(jnp.ones((8, LANES), jnp.bfloat16), marks)
+    ends = jnp.dot(per_row.astype(jnp.bfloat16), upto, preferred_element_type=jnp.float32)
+    starts = (ends - per_row)[:1]
+    ends = ends[:1]
+    crossing = jnp.max(ends).astype(jnp.int32)
+    table[...] = jnp.zeros(table.shape, jnp.bfloat16)
+    fields = [
+        rank[:SLABS] * owned,
+        (local_id & 255).astype(jnp.float32),
+        (local_id >> 8).astype(jnp.float32),
+        partner,
+    ]
+    for k, field in enumerate(fields):
+        table[pl.ds(0, SLABS), pl.ds(k * LANES, LANES)] = field.astype(jnp.bfloat16)
+
+    mine = jnp.sum(got_ref[:, 8:12, :], axis=0)
+    item_row, item_lane = iota((ROWS, LANES), 0), iota((ROWS, LANES), 1)
+    placed = jnp.zeros((ROWS, LANES), jnp.float32)
+    for q in range(ROWS_DEV):
+        placed = jnp.where(item_row == row_owner * ROWS_DEV + q, mine[q : q + 1], placed)
+    counts[pl.ds(0, ROWS), pl.ds(OWNED, ROWS)] = placed.T
+    counts[pl.ds(ROWS, 16), pl.ds(OWNED, ROWS)] = jnp.zeros((16, ROWS), jnp.float32)
+
+    slot_lane = iota((LANES, LANES), 1)
+    col_ids = iota((LANES, COLS), 1, jnp.float32)
+
+    def chunk(step, carry):
+        slot = (step * LANES + iota((LANES, LANES), 0)).astype(jnp.float32)
+        here = (slot >= starts) & (slot < ends)
+        first = jnp.sum(jnp.where(here, starts, 0.0), axis=1, keepdims=True)
+        got = jnp.dot(hot(here).astype(jnp.bfloat16), table[...], preferred_element_type=jnp.float32)
+        chosen = got[:, :LANES] == slot[:, :1] + 1.0 - first
+        ident = got[:, LANES : 2 * LANES] + 256.0 * got[:, 2 * LANES : 3 * LANES]
+        column = jnp.sum(jnp.where(chosen, ident + 1.0, 0.0), axis=1, keepdims=True) - 1.0
+        at = jnp.sum(jnp.where(chosen, slot_lane, 0), axis=1, keepdims=True)
+        reach = LANES - WINDOW
+        other_side = jnp.where(
+            at < LANES // 2, hot(slot_lane >= reach + at), hot(slot_lane <= at - reach)
+        )
+        near = jnp.where(other_side > 0.0, got[:, 3 * LANES :], NONE).T
+        near = jnp.concatenate([near[:16], near[LANES - 16 :]], axis=0)
+        pairs = count_pairs(near, (15, 16))
+        column_hot = hot(column == col_ids).astype(jnp.bfloat16)
+        counts[...] += jnp.dot(pairs, column_hot, preferred_element_type=jnp.float32)
+        return carry
+
+    lax.fori_loop(0, (crossing + LANES - 1) // LANES, chunk, 0)
+
+    margins = jnp.sum(got_ref[:, 12, :], axis=0, keepdims=True)
+    held = jnp.where(item_row == item_lane, margins, 0.0)
+    item_rows = item_row.astype(jnp.float32)
+    for s in range(SLABS):
+        held += jnp.where(items[s : s + 1] == item_rows, cross[s : s + 1], 0.0)
+    row_margin = jnp.sum(held, axis=1, keepdims=True)
+    totals = jnp.sum(got_ref[:, 13, :], axis=0, keepdims=True) + jnp.sum(cross, axis=0, keepdims=True)
+    pair_total = jnp.sum(totals, axis=1, keepdims=True)
+    col_margin = jnp.concatenate(
+        [counts[pl.ds(ROWS, 1), pl.ds(0, OWNED)], jnp.sum(held.T, axis=0, keepdims=True)], axis=1
+    )
+    positive = ppmi(counts[pl.ds(0, ROWS), :], row_margin, col_margin, pair_total)
+    copy.wait()
+    fill_signs(jnp.concatenate([words[...], row_bits_ref[...]], axis=1), signs)
+    result = project(positive, signs)
+    result = jnp.where(overflow > 0.0, jnp.nan, result)
+    for s in range(SLABS):
+        out_ref[s] = result[s * ROWS_DEV : (s + 1) * ROWS_DEV]
+
+
+def route(where, items, sessions, interpret=False):
+    return pl.pallas_call(
+        lambda *refs: route_kernel(where, *refs),
+        out_shape=jax.ShapeDtypeStruct((SLABS, MESSAGE, LANES), jnp.float32),
+        in_specs=[pl.BlockSpec(memory_space=pltpu.HBM)] * 2,
+        out_specs=pl.BlockSpec(memory_space=pltpu.VMEM),
+        scratch_shapes=[
+            pltpu.VMEM((SLAB_ROWS, LANES), jnp.int32),
+            pltpu.VMEM((SLAB_ROWS, LANES), jnp.int32),
+            pltpu.VMEM((2 * PAD + SLAB_ROWS, LANES), jnp.float32),
+            pltpu.VMEM((LANES, 6 * LANES), jnp.bfloat16),
+            pltpu.VMEM((SLABS * QUOTA, LANES), jnp.float32),
+            pltpu.VMEM((ROWS, SLAB_ROWS * LANES), jnp.bfloat16),
+            pltpu.VMEM((ROWS, SLAB_ROWS * LANES), jnp.bfloat16),
+            pltpu.SemaphoreType.DMA((2,)),
+        ],
+        compiler_params=pltpu.CompilerParams(vmem_limit_bytes=VMEM_BYTES),
+        interpret=interpret,
+        name="route_events",
+    )(items, sessions)
+
+
+def sketch_part(where, got, bits, interpret=False):
+    return pl.pallas_call(
+        lambda *refs: sketch_kernel(where, *refs),
+        out_shape=jax.ShapeDtypeStruct((SLABS, ROWS_DEV, SKETCH), jnp.float32),
+        grid=(1,),
+        in_specs=[
+            pl.BlockSpec((SLABS, MESSAGE, LANES), lambda i: (0, 0, 0)),
+            pl.BlockSpec((WORDS, LANES), lambda i: (0, 0)),
+            pl.BlockSpec(memory_space=pltpu.HBM),
+        ],
+        out_specs=pl.BlockSpec((SLABS, ROWS_DEV, SKETCH), lambda i: (0, 0, 0)),
+        scratch_shapes=[
+            pltpu.VMEM((ROWS + 16, COLS), jnp.float32),
+            pltpu.VMEM((LANES, 4 * LANES), jnp.bfloat16),
+            pltpu.VMEM((WORDS, OWNED), jnp.int32),
+            pltpu.VMEM((16 * WORD_BITS, COLS), jnp.bfloat16),
+            pltpu.SemaphoreType.DMA,
+        ],
+        compiler_params=pltpu.CompilerParams(vmem_limit_bytes=VMEM_BYTES),
+        interpret=interpret,
         name="sketch_part",
-    )(own, other, bits)
-
-
-def local(event_items, event_sessions, sketch_bits):
-    def where():
-        return lax.axis_index("stream"), lax.axis_index("item")
-
-    message = pack(
-        where,
-        event_items.reshape(SLAB_ROWS, LANES),
-        event_sessions.reshape(SLAB_ROWS, LANES),
-        sketch_bits,
-    )
-    own = lax.all_to_all(message, "stream", 0, 0, tiled=True)
-    other = lax.ppermute(own, "item", [(i, i ^ 1) for i in range(BANDS)])
-    part = sketch_part(where, own, other, sketch_bits)
+    )(got, bits, bits)
+
+
+def reduced(part):
     rows = jnp.sum(lax.all_to_all(part, "stream", 0, 0, tiled=True), axis=0)
     spread = jnp.broadcast_to(rows[None], (BANDS,) + rows.shape)
     summed = jnp.sum(lax.all_to_all(spread, "item", 0, 0, tiled=True), axis=0)
     return summed / math.sqrt(EVENT_ROWS * LANES)
 
 
+def local(event_items, event_sessions, sketch_bits):
+    def where():
+        return lax.axis_index("stream"), lax.axis_index("item")
+
+    items = event_items.reshape(SLAB_ROWS, LANES)
+    sessions = event_sessions.reshape(SLAB_ROWS, LANES)
+
+    def from_every_event(_):
+        message = all_events(where, items, sessions, sketch_bits)
+        own = lax.all_to_all(message, "stream", 0, 0, tiled=True)
+        other = lax.ppermute(own, "item", [(i, i ^ 1) for i in range(BANDS)])
+        return reduced(from_all(where, own, other, sketch_bits))
+
+    routed = lax.all_to_all(route(where, items, sessions), "stream", 0, 0, tiled=True)
+    result = reduced(sketch_part(where, routed, sketch_bits))
+    return lax.cond(jnp.isnan(result[0, 0]), from_every_event, lambda kept: kept, result)
+
+
 def solution(mesh):
     placed = (P("stream"), P("stream"), P(None, "item"))
     return jax.shard_map(

time: 72.4 us -> 64.4 us (0.89)
  blocking collectives: 51 us -> 36.9 us
  starting transfers between devices: 2.39 us -> 7.36 us
  waiting for transfers between devices: 1.54 us -> 4.72 us
  Pallas kernels: 13.4 us -> 11.7 us
  between operations: 0.03 us -> 1.36 us
  local copies, waits for them, and re-layouts: 3.04 us -> 1.72 us
    all_to_all x3 -> x2, blocking collectives: 51 us -> 36.9 us  [the longest x1 23 us: local(): lax.all_to_all(route(where, items, sessions), 'stream', 0, 0, tiled=True)]
    all_to_all x0 -> x1, starting transfers between devices: none -> 7.36 us  [reduced(): summed = jnp.sum(lax.all_to_all(spread, 'item', 0, 0, tiled=True), axis=0)]
    pallas_call x1, Pallas kernels: 12.9 us -> 5.91 us  [sketch_part(): pl.pallas_call(lambda *refs: sketch_kernel(where, *refs), out_shape=jax.S...]
    pallas_call x1, Pallas kernels: 0.52 us -> 5.82 us  [route(): pl.pallas_call(lambda *refs: route_kernel(where, *refs), out_shape=jax.Sh...]
    all_to_all x0 -> x1, waiting for transfers between devices: none -> 4.72 us  [reduced(): summed = jnp.sum(lax.all_to_all(spread, 'item', 0, 0, tiled=True), axis=0)]
    unnamed x8, local copies, waits for them, and re-layouts: 3.03 us -> 0.6 us
    ppermute x1 -> x0, starting transfers between devices: 2.39 us -> none  [local(): other = lax.ppermute(own, 'item', [(i, i ^ 1) for i in range(BANDS)])]
    ppermute x1 -> x0, waiting for transfers between devices: 1.54 us -> none  [local(): other = lax.ppermute(own, 'item', [(i, i ^ 1) for i in range(BANDS)])]
where the time goes in v2:
time: 64.4 us; the launch traced here: 64.1 us
  blocking collectives  36.9 us (57%)
  Pallas kernels  11.7 us (18%)
  starting transfers between devices  7.36 us (11%)
  waiting for transfers between devices  4.72 us (7%)
  local copies, waits for them, and re-layouts  1.72 us (3%)
  between operations  1.36 us (2%)
    all_to_all x1, blocking collectives, local(): lax.all_to_all(route(where, items, sessions), 'stream', 0, 0, tiled=True)  23 us
    all_to_all x1, blocking collectives, reduced(): rows = jnp.sum(lax.all_to_all(part, 'stream', 0, 0, tiled=True), axis=0)  13.9 us
    all_to_all x1, starting transfers between devices, reduced(): summed = jnp.sum(lax.all_to_all(spread, 'item', 0, 0, tiled=True), axis=0)  7.36 us
    pallas_call x1, Pallas kernels, sketch_part(): pl.pallas_call(lambda *refs: sketch_kernel(where, *refs), out_shape=jax.S...  5.91 us
    pallas_call x1, Pallas kernels, route(): pl.pallas_call(lambda *refs: route_kernel(where, *refs), out_shape=jax.Sh...  5.82 us
    all_to_all x1, waiting for transfers between devices, reduced(): summed = jnp.sum(lax.all_to_all(spread, 'item', 0, 0, tiled=True), axis=0)  4.72 us
  transfers between devices with their start and end apart: 1, of which 1 were waited for; matrix products, arithmetic and copies ran while one was open for 0% of the time, Pallas kernels for 0%

profile of v2, /device:TPU:1, one launch (start us, length us, event | category | flops | bytes accessed | tf_op | source)
XLA Modules:
  0.0 64.1 jit_solution(5512196627715669703)
XLA Ops:
  0.0 5.8 %route_events.1 = f32[32,16,128]{2,1,0:T(8,128)S(1)} custom-call(s32[32,128]{1,0:T(8,128)} %bitcast.3, s32[32,128]{1,0:T(8,128)} %bitcast.5), custom_call_target="tpu_custom_call" | custom-call | tf_op jit(solution)/shard_map/route_events/pallas_call | solution.py:593
  5.8 23.0 %all_to_all.30.refs_0_ = f32[32,16,128]{2,1,0:T(8,128)S(1)} all-to-all(f32[32,16,128]{2,1,0:T(8,128)S(1)} %route_events.1), channel_id=1, replica_groups=mesh['stream'=32,'item'=8] {'stream'}, dimensions={0} | all-to-all | bytes 524288 | tf_op jit(solution)/shard_map/all_to_all | solution.py:658
  28.9 0.0 copy-start
  28.9 0.0 copy-start.1
  28.9 0.0 copy-start.2
  28.9 5.9 %sketch_part.1 = f32[32,4,256]{2,1,0:T(4,128)S(1)} custom-call(f32[32,16,128]{2,1,0:T(8,128)S(1)} %all_to_all.30.refs_0_, s32[15,32768]{1,0:T(8,128)} %refs_2_.1, s32[15,32768]{1,0:T(8,128)} %refs_2_.1), custom_call_target="tpu_custom_call" | custom-call | tf_op jit(solution)/shard_map/sketch_part/pallas_call | solution.py:615
  34.8 13.9 %all_to_all.31 = f32[32,4,256]{2,1,0:T(4,128)S(1)} all-to-all(f32[32,4,256]{2,1,0:T(4,128)S(1)} %sketch_part.1), channel_id=1, replica_groups=mesh['stream'=32,'item'=8] {'stream'}, dimensions={0} | all-to-all | bytes 262144 | tf_op jit(solution)/shard_map/all_to_all | solution.py:639
  48.7 0.6 broadcast_in_dim.4
  49.3 7.4 %all-to-all-start.5 = ((f32[8,4,256]{2,1,0:T(4,128)}), f32[8,4,256]{2,1,0:T(4,128)S(1)}, u32[]{:S(2)}, u32[]{:S(2)}) async-start(f32[8,4,256]{2,1,0:T(4,128)} %broadcast_in_dim.4), calls=%async_computation.5 | async-start | bytes 65536 | tf_op jit(solution)/shard_map/all_to_all | solution.py:641
  56.7 4.7 %all-to-all-done.5 = f32[8,4,256]{2,1,0:T(4,128)S(1)} async-done(((f32[8,4,256]{2,1,0:T(4,128)}), f32[8,4,256]{2,1,0:T(4,128)S(1)}, u32[]{:S(2)}, u32[]{:S(2)}) %all-to-all-start.5) | async-done | bytes 32800 | tf_op jit(solution)/shard_map/all_to_all | solution.py:641
  61.5 0.5 slice.4
  63.3 0.0 copy-done
  63.3 0.0 copy-done.1
  63.3 0.0 copy-done.2
  63.3 0.2 conditional.1
  63.5 0.0 copy-start.3
  63.5 0.6 copy-done.3
  (3 shorter events, 0.1 us)
Async XLA Ops:
  28.9 34.4 %copy-start = (s32[15,32768]{1,0:T(8,128)S(1)}, s32[15,32768]{1,0:T(8,128)}, u32[]{:S(2)}) copy-start(s32[15,32768]{1,0:T(8,128)} %refs_2_.1) | copy-start | bytes 5898244
  28.9 34.4 %copy-start.1 = (s32[4096]{0:T(1024)S(1)}, s32[4096]{0:T(1024)}, u32[]{:S(2)}) copy-start(s32[4096]{0:T(1024)} %param.5) | copy-start | bytes 49156
  28.9 34.4 %copy-start.2 = (s32[4096]{0:T(1024)S(1)}, s32[4096]{0:T(1024)}, u32[]{:S(2)}) copy-start(s32[4096]{0:T(1024)} %param.6) | copy-start | bytes 49156
  49.3 12.1 %all-to-all-start.5 = ((f32[8,4,256]{2,1,0:T(4,128)}), f32[8,4,256]{2,1,0:T(4,128)S(1)}, u32[]{:S(2)}, u32[]{:S(2)}) async-start(f32[8,4,256]{2,1,0:T(4,128)} %broadcast_in_dim.4), calls=%async_computation.5 | async-start | bytes 65536 | tf_op jit(solution)/shard_map/all_to_all | solution.py:641
  63.5 0.6 copy-start.3

commit v3 on v2

--- a/solution.py
+++ b/solution.py
@@ -26,9 +26,13 @@
 PAD = 8
 MARGIN_ROW, TOTAL_ROW, BITS_ROW = 24, 25, 26
 QUOTA = 32
-MESSAGE = 16
+MESSAGE = 8
+HALF = LANES // 2
 NONE = 255.0
+NOBODY = 4095.0
+SPOT = HALF + 16
 VMEM_BYTES = 48 << 20
+COUNT = jnp.bfloat16
 
 
 def iota(shape, axis, dtype=jnp.int32):
@@ -62,6 +66,12 @@
     mid = rest.astype(jnp.bfloat16)
     low = (rest - mid.astype(jnp.float32)).astype(jnp.bfloat16)
     return jnp.concatenate([high, mid, low], axis=0)
+
+
+def two_parts(values):
+    high = values.astype(jnp.bfloat16)
+    low = (values - high.astype(jnp.float32)).astype(jnp.bfloat16)
+    return jnp.concatenate([high, low], axis=0)
 
 
 def joined(parts):
@@ -391,19 +401,29 @@
         per_row = jnp.where(lane == r, ranks[r][:, LANES - 1 :], per_row)
     ends = jnp.dot(per_row.astype(jnp.bfloat16), upto, preferred_element_type=jnp.float32)
     starts = ends - per_row
-    most = jnp.max(ends[:, LANES - 1 :], axis=0, keepdims=True)
+    block = jnp.where(items >= ROWS, items >> 10, -1)
+    sixteen = iota((16, LANES), 0)
+    upper = [hot((block[r : r + 1] >> 4) == sixteen) for r in range(SLAB_ROWS)]
+    lower = [hot((block[r : r + 1] & 15) == sixteen) for r in range(SLAB_ROWS)]
+    loads = nt_dot(
+        jnp.concatenate(upper, axis=1).astype(jnp.bfloat16),
+        jnp.concatenate(lower, axis=1).astype(jnp.bfloat16),
+    )
+    most = jnp.max(jnp.max(loads, axis=0, keepdims=True), axis=1, keepdims=True)
     orders = [
         jnp.sum(marks[r] * (ranks[r] + starts[:, r : r + 1]), axis=0, keepdims=True)
         for r in range(SLAB_ROWS)
     ]
-    table[pl.ds(SLAB_ROWS, LANES - SLAB_ROWS), :] = jnp.zeros((LANES - SLAB_ROWS, 6 * LANES), jnp.bfloat16)
+    table[pl.ds(SLAB_ROWS, LANES - SLAB_ROWS), :] = jnp.zeros((LANES - SLAB_ROWS, 5 * LANES), jnp.bfloat16)
+    row_codes = codes[pl.ds(PAD, SLAB_ROWS), :]
+    left = jnp.where(lane >= LANES - 32, codes[pl.ds(PAD - 1, SLAB_ROWS), :], row_codes)
+    right = jnp.where(lane < 32, codes[pl.ds(PAD + 1, SLAB_ROWS), :], row_codes)
     fields = [
         jnp.minimum(jnp.concatenate(orders, axis=0), 255.0),
         (inside & 255).astype(jnp.float32),
         (inside >> 8).astype(jnp.float32),
-        codes[pl.ds(PAD - 1, SLAB_ROWS), :],
-        codes[pl.ds(PAD, SLAB_ROWS), :],
-        codes[pl.ds(PAD + 1, SLAB_ROWS), :],
+        pltpu.roll(left, 32, 1),
+        pltpu.roll(right, LANES - 32, 1),
     ]
     for k, field in enumerate(fields):
         table[pl.ds(0, SLAB_ROWS), pl.ds(k * LANES, LANES)] = field.astype(jnp.bfloat16)
@@ -420,15 +440,12 @@
     ordinal = ((number & (QUOTA - 1)) + 1).astype(jnp.float32)
     chosen = (got[:, :LANES] == ordinal) & (high >= 0.0) & (high < 4.0)
     ident = got[:, LANES : 2 * LANES] + 256.0 * high
-    column = jnp.sum(jnp.where(chosen, ident + 1.0, 0.0), axis=1, keepdims=True) - 1.0
-    at_lane = jnp.sum(jnp.where(chosen, lanes.astype(jnp.float32), 0.0), axis=1, keepdims=True)
-    source = at_lane.astype(jnp.int32) + (lanes - WINDOW)
-    index = source & (LANES - 1)
-    parts = [
-        jnp.take_along_axis(got[:, k * LANES : (k + 1) * LANES], index, axis=1, mode="promise_in_bounds")
-        for k in (3, 4, 5)
-    ]
-    window = jnp.where(source < 0, parts[0], jnp.where(source < LANES, parts[1], parts[2]))
+    column = NOBODY + jnp.sum(jnp.where(chosen, ident - NOBODY, 0.0), axis=1, keepdims=True)
+    at_lane = jnp.sum(jnp.where(chosen, lanes, 0), axis=1, keepdims=True)
+    in_left = at_lane < HALF
+    index = (at_lane + jnp.where(in_left, 32 - WINDOW, -32 - WINDOW) + lanes) & (LANES - 1)
+    reach = jnp.where(in_left, got[:, 3 * LANES : 4 * LANES], got[:, 4 * LANES :])
+    window = jnp.take_along_axis(reach, index, axis=1, mode="promise_in_bounds")
     from_lane, to_lane = iota((LANES, LANES), 0), iota((LANES, LANES), 1)
     ahead = (to_lane > WINDOW) & (from_lane > WINDOW) & (from_lane <= to_lane)
     behind = (to_lane < WINDOW) & (from_lane > to_lane) & (from_lane <= WINDOW)
@@ -438,85 +455,84 @@
     )
     linked = (crossed == 0.0) & (lanes <= 2 * WINDOW)
     near = jnp.where(linked, jnp.abs(window) - 1.0, NONE)
-    near_rows[...] = jnp.where(lanes == WINDOW, column, near)
-
+    near = jnp.where(lanes == WINDOW, column, near)
+    near_rows[...] = (near + 4096.0 * pltpu.roll(near, LANES - 16, 1)).astype(jnp.int32)
+
+    whole = jnp.where(item_row == iota((ROWS, LANES), 1), ordered, row_pairs).astype(jnp.int32)
+    packed = pltpu.roll(whole, HALF, 1) + jnp.where(iota((ROWS, LANES), 1) >= HALF, whole * 65536, 0)
     ends_lane = iota((1, LANES), 1)
-    spare = jnp.where(most > QUOTA, 1.0, 0.0)
-    edge_items = jnp.where(ends_lane < LANES // 2, items[:1], items[SLAB_ROWS - 1 :]).astype(jnp.float32)
-    edge_items = jnp.where(ends_lane == LANES // 2, spare, edge_items)
-    edge_sessions = jnp.where(
-        ends_lane < LANES // 2, sessions[:1], sessions[SLAB_ROWS - 1 :]
-    ).astype(jnp.float32)
-    common = jnp.concatenate([margin, total, edge_items, edge_sessions], axis=0)
-    quarter = iota((8, LANES), 1) >> 5
+    spare = jnp.where(most > QUOTA, 1, 0)
+    total = jnp.sum(total, axis=1, keepdims=True).astype(jnp.int32)
+    margin = margin.astype(jnp.int32)
+
+    def edges(values, single):
+        both = jnp.where(ends_lane < LANES - 32, pltpu.roll(values[:1], HALF, 1), values[SLAB_ROWS - 1 :])
+        return jnp.where(ends_lane == SPOT, single, both)
+
+    common = jnp.concatenate(
+        [pltpu.roll(margin, HALF, 1), margin, edges(items, total), edges(sessions, spare)], axis=0
+    )
+    sixteenth = iota((8, LANES), 1) >> 4
     for s in range(SLABS):
-        rows = near_rows[pl.ds(s * QUOTA, 8), :]
-        for g in range(1, QUOTA // 8):
-            part = pltpu.roll(near_rows[pl.ds(s * QUOTA + 8 * g, 8), :], 32 * g, 1)
-            rows = jnp.where(quarter == g, part, rows)
-        out_ref[s, pl.ds(0, 8), :] = rows
-        out_ref[s, pl.ds(8, 8), :] = jnp.concatenate(
-            [row_pairs[s * ROWS_DEV : (s + 1) * ROWS_DEV], common], axis=0
-        )
+        rows = jnp.concatenate([packed[s * ROWS_DEV : (s + 1) * ROWS_DEV], common], axis=0)
+        for g in range(QUOTA // 8):
+            part = near_rows[pl.ds(s * QUOTA + 8 * g, 8), :]
+            rows = jnp.where(sixteenth == g, pltpu.roll(part, 16 * g, 1) if g else part, rows)
+        out_ref[s] = rows
 
 
 def count_pairs(near, skip):
     slots = near.shape[1]
-    row_ids = iota((ROWS, slots), 0, jnp.float32)
-    pairs = jnp.zeros((ROWS, slots), jnp.float32)
-    for d in range(near.shape[0]):
-        if d not in skip:
-            pairs += hot(near[d : d + 1] == row_ids)
     place = iota(near.shape, 0)
     real = near < NONE
     for d in skip:
         real = real & (place != d)
     weight = jnp.sum(hot(real), axis=0, keepdims=True)
-    return jnp.concatenate([pairs, jnp.broadcast_to(weight, (16, slots))], axis=0).astype(jnp.bfloat16)
-
-
-def sketch_kernel(where, got_ref, row_bits_ref, bits_hbm, out_ref, counts, table, words, signs, sem):
+    row_ids = iota((ROWS, slots), 0, jnp.float32).astype(COUNT)
+    one, none = jnp.ones((), COUNT), jnp.zeros((), COUNT)
+    pairs = jnp.zeros((ROWS, slots), COUNT)
+    near = near.astype(COUNT)
+    for d in range(near.shape[0]):
+        if d not in skip:
+            pairs += jnp.where(near[d : d + 1] == row_ids, one, none)
+    weight = jnp.broadcast_to(weight, (16, slots)).astype(jnp.bfloat16)
+    return jnp.concatenate([pairs.astype(jnp.bfloat16), weight], axis=0)
+
+
+def sketch_kernel(
+    where, got_ref, row_bits_ref, bits_hbm, out_ref, spoilt_ref, counts, table, words, wide_signs, sem
+):
     slab, band = where()
     copy = pltpu.make_async_copy(
         bits_hbm.at[:, pl.ds(pl.multiple_of(slab * OWNED, OWNED), OWNED)], words, sem
     )
     copy.start()
 
-    windows = got_ref[:, :8, :].reshape(SLABS * 8, LANES).T
-    blocks, idents = [], []
-    for g in range(QUOTA // 8):
-        near = windows[32 * g : 32 * g + 32]
-        idents.append(near[WINDOW : WINDOW + 1])
-        blocks.append(count_pairs(near, (WINDOW, 31)))
-    ident = jnp.concatenate(idents, axis=1)
-    pairs = jnp.concatenate(blocks, axis=1)
-    column_hot = hot(ident == iota((OWNED, ident.shape[1]), 0, jnp.float32)).astype(jnp.bfloat16)
-    counts[:, pl.ds(0, OWNED)] = nt_dot(pairs, column_hot)
-
-    edge_items, edge_sessions = got_ref[:, 14, :], got_ref[:, 15, :]
-    overflow = jnp.max(edge_items[:, LANES // 2 : LANES // 2 + 1], axis=0, keepdims=True)
     slab_row, lane = iota((SLABS, LANES), 0), iota((SLABS, LANES), 1)
+    raw_items, raw_sessions = got_ref[:, 6, :], got_ref[:, 7, :]
+    edge_items = jnp.where(lane < HALF, pltpu.roll(raw_items, HALF, 1), raw_items)
+    edge_sessions = jnp.where(lane < HALF, pltpu.roll(raw_sessions, HALF, 1), raw_sessions)
+    spoilt_ref[0, 0] = jnp.max(jnp.where(lane == SPOT, raw_sessions, 0))
     end_items = pltpu.roll(edge_items, 1, 0)
-    end_sess = jnp.where(slab_row == 0, -1.0, pltpu.roll(edge_sessions, 1, 0))
+    end_sess = jnp.where(slab_row == 0, -1, pltpu.roll(edge_sessions, 1, 0))
     cross = jnp.zeros((SLABS, LANES), jnp.float32)
     for d in range(1, WINDOW + 1):
         before = pltpu.roll(end_sess, d, 1)
         after = pltpu.roll(edge_sessions, LANES - d, 1)
         cross += hot((lane < d) & (before == edge_sessions))
         cross += hot((lane >= LANES - d) & (after == end_sess))
-    items = jnp.where(lane < LANES // 2, edge_items, end_items)
+    items = jnp.where(lane < HALF, edge_items, end_items)
     over = jnp.where(
-        lane < LANES // 2,
+        lane < HALF,
         hot((edge_sessions == end_sess[:, LANES - 1 :]) & (lane < WINDOW)),
         hot((end_sess == edge_sessions[:, :1]) & (lane >= LANES - WINDOW)),
     )
-    partner = jnp.where(over > 0.0, jnp.minimum(items, float(ROWS)), NONE)
-    whole = items.astype(jnp.int32)
-    is_row = whole < ROWS
+    partner = jnp.where(over > 0.0, jnp.minimum(items, ROWS).astype(jnp.float32), NONE)
+    is_row = items < ROWS
     row_owner = jnp.where(band == 0, slab, -1)
-    owned = jnp.where(is_row, whole >> 2, whole >> 10) == jnp.where(is_row, row_owner, band * SLABS + slab)
+    owned = jnp.where(is_row, items >> 2, items >> 10) == jnp.where(is_row, row_owner, band * SLABS + slab)
     owned = hot(owned & (cross > 0.0))
-    local_id = jnp.where(is_row, OWNED + whole, whole & (OWNED - 1))
+    local_id = jnp.where(is_row, OWNED + items, items & (OWNED - 1))
     upto = hot(iota((LANES, LANES), 0) <= iota((LANES, LANES), 1)).astype(jnp.bfloat16)
     blank = jnp.zeros((LANES - SLABS, LANES), jnp.float32)
     marks = jnp.concatenate([owned, blank], axis=0).astype(jnp.bfloat16)
@@ -526,7 +542,6 @@
     starts = (ends - per_row)[:1]
     ends = ends[:1]
     crossing = jnp.max(ends).astype(jnp.int32)
-    table[...] = jnp.zeros(table.shape, jnp.bfloat16)
     fields = [
         rank[:SLABS] * owned,
         (local_id & 255).astype(jnp.float32),
@@ -534,20 +549,11 @@
         partner,
     ]
     for k, field in enumerate(fields):
-        table[pl.ds(0, SLABS), pl.ds(k * LANES, LANES)] = field.astype(jnp.bfloat16)
-
-    mine = jnp.sum(got_ref[:, 8:12, :], axis=0)
-    item_row, item_lane = iota((ROWS, LANES), 0), iota((ROWS, LANES), 1)
-    placed = jnp.zeros((ROWS, LANES), jnp.float32)
-    for q in range(ROWS_DEV):
-        placed = jnp.where(item_row == row_owner * ROWS_DEV + q, mine[q : q + 1], placed)
-    counts[pl.ds(0, ROWS), pl.ds(OWNED, ROWS)] = placed.T
-    counts[pl.ds(ROWS, 16), pl.ds(OWNED, ROWS)] = jnp.zeros((16, ROWS), jnp.float32)
-
+        table[:, pl.ds(k * LANES, LANES)] = jnp.concatenate([field, blank], axis=0).astype(jnp.bfloat16)
     slot_lane = iota((LANES, LANES), 1)
     col_ids = iota((LANES, COLS), 1, jnp.float32)
 
-    def chunk(step, carry):
+    def crossed(step):
         slot = (step * LANES + iota((LANES, LANES), 0)).astype(jnp.float32)
         here = (slot >= starts) & (slot < ends)
         first = jnp.sum(jnp.where(here, starts, 0.0), axis=1, keepdims=True)
@@ -557,34 +563,70 @@
         column = jnp.sum(jnp.where(chosen, ident + 1.0, 0.0), axis=1, keepdims=True) - 1.0
         at = jnp.sum(jnp.where(chosen, slot_lane, 0), axis=1, keepdims=True)
         reach = LANES - WINDOW
-        other_side = jnp.where(
-            at < LANES // 2, hot(slot_lane >= reach + at), hot(slot_lane <= at - reach)
-        )
+        other_side = jnp.where(at < HALF, hot(slot_lane >= reach + at), hot(slot_lane <= at - reach))
         near = jnp.where(other_side > 0.0, got[:, 3 * LANES :], NONE).T
         near = jnp.concatenate([near[:16], near[LANES - 16 :]], axis=0)
         pairs = count_pairs(near, (15, 16))
         column_hot = hot(column == col_ids).astype(jnp.bfloat16)
-        counts[...] += jnp.dot(pairs, column_hot, preferred_element_type=jnp.float32)
+        return jnp.dot(pairs, column_hot, preferred_element_type=jnp.float32)
+
+    first_crossed = crossed(0)
+
+    windows = got_ref[...].reshape(SLABS * MESSAGE, LANES).T[:HALF]
+    low, high = (windows & 4095).astype(jnp.float32), (windows >> 12).astype(jnp.float32)
+    blocks, idents = [], []
+    for g in range(QUOTA // 8):
+        near = jnp.concatenate([low[16 * g : 16 * g + 16], high[16 * g : 16 * g + 16]], axis=0)
+        idents.append(near[WINDOW : WINDOW + 1])
+        blocks.append(count_pairs(near, (WINDOW, 31)))
+    ident = jnp.concatenate(idents, axis=1)
+    pairs = jnp.concatenate(blocks, axis=1)
+    column_hot = hot(ident == iota((OWNED, ident.shape[1]), 0, jnp.float32)).astype(jnp.bfloat16)
+    counts[:, pl.ds(0, OWNED)] = nt_dot(pairs, column_hot) + first_crossed[:, :OWNED]
+
+    low_sum = jnp.zeros((MESSAGE, LANES), jnp.int32)
+    high_sum = jnp.zeros((MESSAGE, LANES), jnp.int32)
+    for s in range(SLABS):
+        word = got_ref[s]
+        low_sum += word & 65535
+        high_sum += (word >> 16) & 65535
+    mine = jnp.where(iota((MESSAGE, LANES), 1) < HALF, pltpu.roll(low_sum, HALF, 1), high_sum)
+    item_row, item_lane = iota((ROWS, LANES), 0), iota((ROWS, LANES), 1)
+    placed = jnp.zeros((ROWS, LANES), jnp.int32)
+    for q in range(ROWS_DEV):
+        placed = jnp.where(item_row == row_owner * ROWS_DEV + q, mine[q : q + 1], placed)
+    placed = jnp.where(item_row == item_lane, 2 * placed, placed).astype(jnp.float32)
+    counts[pl.ds(0, ROWS), pl.ds(OWNED, ROWS)] = placed.T + first_crossed[:ROWS, OWNED:]
+
+    def chunk(step, carry):
+        counts[...] += crossed(step)
         return carry
 
-    lax.fori_loop(0, (crossing + LANES - 1) // LANES, chunk, 0)
-
-    margins = jnp.sum(got_ref[:, 12, :], axis=0, keepdims=True)
-    held = jnp.where(item_row == item_lane, margins, 0.0)
-    item_rows = item_row.astype(jnp.float32)
+    lax.fori_loop(1, (crossing + LANES - 1) // LANES, chunk, 0)
+
+    margin_low = jnp.sum(got_ref[:, 4, :], axis=0, keepdims=True)
+    margin_high = jnp.sum(got_ref[:, 5, :], axis=0, keepdims=True)
+    margins = jnp.where(item_lane[:1] < HALF, pltpu.roll(margin_low, HALF, 1), margin_high)
+    held = jnp.where(item_row == item_lane, margins.astype(jnp.float32), 0.0)
     for s in range(SLABS):
-        held += jnp.where(items[s : s + 1] == item_rows, cross[s : s + 1], 0.0)
+        held += jnp.where(items[s : s + 1] == item_row, cross[s : s + 1], 0.0)
     row_margin = jnp.sum(held, axis=1, keepdims=True)
-    totals = jnp.sum(got_ref[:, 13, :], axis=0, keepdims=True) + jnp.sum(cross, axis=0, keepdims=True)
-    pair_total = jnp.sum(totals, axis=1, keepdims=True)
+    totals = jnp.where(lane == SPOT, raw_items, 0).astype(jnp.float32) + cross
+    pair_total = jnp.sum(jnp.sum(totals, axis=0, keepdims=True), axis=1, keepdims=True)
     col_margin = jnp.concatenate(
         [counts[pl.ds(ROWS, 1), pl.ds(0, OWNED)], jnp.sum(held.T, axis=0, keepdims=True)], axis=1
     )
     positive = ppmi(counts[pl.ds(0, ROWS), :], row_margin, col_margin, pair_total)
     copy.wait()
-    fill_signs(jnp.concatenate([words[...], row_bits_ref[...]], axis=1), signs)
-    result = project(positive, signs)
-    result = jnp.where(overflow > 0.0, jnp.nan, result)
+    held_words = jnp.concatenate([words[...], row_bits_ref[...]], axis=1)
+    for b in range(WORD_BITS):
+        sign = jnp.where((held_words >> b) & 1 == 1, 1.0, -1.0)
+        for j in range(COLS // LANES):
+            wide_signs[j, pl.ds(b, WORDS, stride=WORD_BITS), :] = sign[:, j * LANES : (j + 1) * LANES]
+    parts = two_parts(positive)
+    signs = [wide_signs[j, pl.ds(0, SKETCH), :].astype(jnp.bfloat16) for j in range(COLS // LANES)]
+    result = nt_dot(parts, jnp.concatenate(signs, axis=1))
+    result = result[:ROWS] + result[ROWS:]
     for s in range(SLABS):
         out_ref[s] = result[s * ROWS_DEV : (s + 1) * ROWS_DEV]
 
@@ -592,15 +634,15 @@
 def route(where, items, sessions, interpret=False):
     return pl.pallas_call(
         lambda *refs: route_kernel(where, *refs),
-        out_shape=jax.ShapeDtypeStruct((SLABS, MESSAGE, LANES), jnp.float32),
+        out_shape=jax.ShapeDtypeStruct((SLABS, MESSAGE, LANES), jnp.int32),
         in_specs=[pl.BlockSpec(memory_space=pltpu.HBM)] * 2,
         out_specs=pl.BlockSpec(memory_space=pltpu.VMEM),
         scratch_shapes=[
             pltpu.VMEM((SLAB_ROWS, LANES), jnp.int32),
             pltpu.VMEM((SLAB_ROWS, LANES), jnp.int32),
             pltpu.VMEM((2 * PAD + SLAB_ROWS, LANES), jnp.float32),
-            pltpu.VMEM((LANES, 6 * LANES), jnp.bfloat16),
-            pltpu.VMEM((SLABS * QUOTA, LANES), jnp.float32),
+            pltpu.VMEM((LANES, 5 * LANES), jnp.bfloat16),
+            pltpu.VMEM((SLABS * QUOTA, LANES), jnp.int32),
             pltpu.VMEM((ROWS, SLAB_ROWS * LANES), jnp.bfloat16),
             pltpu.VMEM((ROWS, SLAB_ROWS * LANES), jnp.bfloat16),
             pltpu.SemaphoreType.DMA((2,)),
@@ -614,19 +656,25 @@
 def sketch_part(where, got, bits, interpret=False):
     return pl.pallas_call(
         lambda *refs: sketch_kernel(where, *refs),
-        out_shape=jax.ShapeDtypeStruct((SLABS, ROWS_DEV, SKETCH), jnp.float32),
+        out_shape=(
+            jax.ShapeDtypeStruct((SLABS, ROWS_DEV, SKETCH), jnp.float32),
+            jax.ShapeDtypeStruct((1, 1), jnp.int32),
+        ),
         grid=(1,),
         in_specs=[
             pl.BlockSpec((SLABS, MESSAGE, LANES), lambda i: (0, 0, 0)),
             pl.BlockSpec((WORDS, LANES), lambda i: (0, 0)),
             pl.BlockSpec(memory_space=pltpu.HBM),
         ],
-        out_specs=pl.BlockSpec((SLABS, ROWS_DEV, SKETCH), lambda i: (0, 0, 0)),
+        out_specs=(
+            pl.BlockSpec((SLABS, ROWS_DEV, SKETCH), lambda i: (0, 0, 0)),
+            pl.BlockSpec(memory_space=pltpu.SMEM),
+        ),
         scratch_shapes=[
             pltpu.VMEM((ROWS + 16, COLS), jnp.float32),
             pltpu.VMEM((LANES, 4 * LANES), jnp.bfloat16),
             pltpu.VMEM((WORDS, OWNED), jnp.int32),
-            pltpu.VMEM((16 * WORD_BITS, COLS), jnp.bfloat16),
+            pltpu.VMEM((COLS // LANES, 16 * WORD_BITS, LANES), jnp.float32),
             pltpu.SemaphoreType.DMA,
         ],
         compiler_params=pltpu.CompilerParams(vmem_limit_bytes=VMEM_BYTES),
@@ -635,11 +683,10 @@
     )(got, bits, bits)
 
 
-def reduced(part):
+def shares(part):
     rows = jnp.sum(lax.all_to_all(part, "stream", 0, 0, tiled=True), axis=0)
     spread = jnp.broadcast_to(rows[None], (BANDS,) + rows.shape)
-    summed = jnp.sum(lax.all_to_all(spread, "item", 0, 0, tiled=True), axis=0)
-    return summed / math.sqrt(EVENT_ROWS * LANES)
+    return lax.all_to_all(spread, "item", 0, 0, tiled=True)
 
 
 def local(event_items, event_sessions, sketch_bits):
@@ -653,11 +700,12 @@
         message = all_events(where, items, sessions, sketch_bits)
         own = lax.all_to_all(message, "stream", 0, 0, tiled=True)
         other = lax.ppermute(own, "item", [(i, i ^ 1) for i in range(BANDS)])
-        return reduced(from_all(where, own, other, sketch_bits))
+        return shares(from_all(where, own, other, sketch_bits))
 
     routed = lax.all_to_all(route(where, items, sessions), "stream", 0, 0, tiled=True)
-    result = reduced(sketch_part(where, routed, sketch_bits))
-    return lax.cond(jnp.isnan(result[0, 0]), from_every_event, lambda kept: kept, result)
+    part, spoilt = sketch_part(where, routed, sketch_bits)
+    gathered = lax.cond(spoilt[0, 0] > 0, from_every_event, lambda kept: kept, shares(part))
+    return jnp.sum(gathered, axis=0) / math.sqrt(EVENT_ROWS * LANES)
 
 
 def solution(mesh):

time: 64.4 us -> 58.3 us (0.905)
  blocking collectives: 36.9 us -> 33.8 us
  Pallas kernels: 11.7 us -> 10.1 us
  local copies, waits for them, and re-layouts: 1.72 us -> 0.62 us
  between operations: 1.36 us -> 0.69 us
  waiting for transfers between devices: 4.72 us -> 4.07 us
    all_to_all x1, blocking collectives: 23 us -> 21.2 us  [local(): lax.all_to_all(route(where, items, sessions), 'stream', 0, 0, tiled=True)]
    pallas_call x1, Pallas kernels: 5.91 us -> 4.55 us  [sketch_part(): pl.pallas_call(lambda *refs: sketch_kernel(where, *refs), out_shape=(jax....]
    all_to_all x1, blocking collectives: 13.9 us -> 12.6 us  [shares(): rows = jnp.sum(lax.all_to_all(part, 'stream', 0, 0, tiled=True), axis=0)]
    all_to_all x1, waiting for transfers between devices: 4.72 us -> 4.07 us  [shares(): return lax.all_to_all(spread, 'item', 0, 0, tiled=True)]
where the time goes in v3:
time: 58.3 us; the launch traced here: 57.9 us
  blocking collectives  33.8 us (58%)
  Pallas kernels  10.1 us (17%)
  starting transfers between devices  7.63 us (13%)
  waiting for transfers between devices  4.07 us (7%)
  between operations  0.69 us (1%)
  other arithmetic  0.66 us (1%)
  local copies, waits for them, and re-layouts  0.62 us (1%)
    all_to_all x1, blocking collectives, local(): lax.all_to_all(route(where, items, sessions), 'stream', 0, 0, tiled=True)  21.2 us
    all_to_all x1, blocking collectives, shares(): rows = jnp.sum(lax.all_to_all(part, 'stream', 0, 0, tiled=True), axis=0)  12.6 us
    all_to_all x1, starting transfers between devices, shares(): return lax.all_to_all(spread, 'item', 0, 0, tiled=True)  7.63 us
    pallas_call x1, Pallas kernels, route(): pl.pallas_call(lambda *refs: route_kernel(where, *refs), out_shape=jax.Sh...  5.59 us
    pallas_call x1, Pallas kernels, sketch_part(): pl.pallas_call(lambda *refs: sketch_kernel(where, *refs), out_shape=(jax....  4.55 us
    all_to_all x1, waiting for transfers between devices, shares(): return lax.all_to_all(spread, 'item', 0, 0, tiled=True)  4.07 us
  transfers between devices with their start and end apart: 1, of which 1 were waited for; matrix products, arithmetic and copies ran while one was open for 0% of the time, Pallas kernels for 0%

profile of v3, /device:TPU:1, one launch (start us, length us, event | category | flops | bytes accessed | tf_op | source)
XLA Modules:
  0.0 57.9 jit_solution(11385250962344644412)
XLA Ops:
  0.0 5.6 %route_events.1 = s32[32,8,128]{2,1,0:T(8,128)S(1)} custom-call(s32[32,128]{1,0:T(8,128)} %bitcast.3, s32[32,128]{1,0:T(8,128)} %bitcast.5), custom_call_target="tpu_custom_call" | custom-call | tf_op jit(solution)/shard_map/route_events/pallas_call | solution.py:635
  5.6 21.2 %all_to_all.33.refs_0_ = s32[32,8,128]{2,1,0:T(8,128)S(1)} all-to-all(s32[32,8,128]{2,1,0:T(8,128)S(1)} %route_events.1), channel_id=1, replica_groups=mesh['stream'=32,'item'=8] {'stream'}, dimensions={0} | all-to-all | bytes 262144 | tf_op jit(solution)/shard_map/all_to_all | solution.py:705
  26.8 0.0 copy-start
  26.8 0.0 copy-start.1
  26.8 0.0 copy-start.2
  26.8 4.6 %sketch_part.1 = (f32[32,4,256]{2,1,0:T(4,128)S(1)}, s32[1,1]{1,0:T(1,128)}) custom-call(s32[32,8,128]{2,1,0:T(8,128)S(1)} %all_to_all.33.refs_0_, s32[15,32768]{1,0:T(8,128)} %refs_2_.1, s32[15,32768]{1,0:T(8,128)} %refs_2_.1), custom_call_target="tpu_custom_call" | custom-call | tf_op jit(solution)/shard_map/sketch_part/pallas_call | solution.py:657
  31.4 12.6 %all_to_all.34 = f32[32,4,256]{2,1,0:T(4,128)S(1)} all-to-all(f32[32,4,256]{2,1,0:T(4,128)S(1)} %get-tuple-element.27), channel_id=1, replica_groups=mesh['stream'=32,'item'=8] {'stream'}, dimensions={0} | all-to-all | bytes 262144 | tf_op jit(solution)/shard_map/all_to_all | solution.py:687
  44.0 0.6 %broadcast_in_dim.4 = f32[8,4,256]{2,1,0:T(4,128)} broadcast(f32[4,256]{1,0:T(4,128)S(1)} %reduce_sum.33), dimensions={1,2} | broadcast | bytes 36864 | tf_op jit(solution)/shard_map/broadcast_in_dim | solution.py:688
  44.7 7.6 %all-to-all-start.5 = ((f32[8,4,256]{2,1,0:T(4,128)}), f32[8,4,256]{2,1,0:T(4,128)S(1)}, u32[]{:S(2)}, u32[]{:S(2)}) async-start(f32[8,4,256]{2,1,0:T(4,128)} %broadcast_in_dim.4), calls=%async_computation.5 | async-start | bytes 65536 | tf_op jit(solution)/shard_map/all_to_all | solution.py:689
  52.9 4.1 %all-to-all-done.5 = f32[8,4,256]{2,1,0:T(4,128)S(1)} async-done(((f32[8,4,256]{2,1,0:T(4,128)}), f32[8,4,256]{2,1,0:T(4,128)S(1)}, u32[]{:S(2)}, u32[]{:S(2)}) %all-to-all-start.5) | async-done | bytes 32800 | tf_op jit(solution)/shard_map/all_to_all | solution.py:689
  57.0 0.0 copy-done
  57.0 0.0 copy-done.1
  57.0 0.0 copy-done.2
  57.0 0.3 conditional.1
  57.3 0.6 %broadcast_multiply_fusion = f32[4,256]{1,0:T(4,128)} fusion(f32[4,256]{1,0:T(4,128)S(1)} %get-tuple-element.28), kind=kLoop, calls=%fused_computation | loop fusion | flops 1024 | bytes 8192 | tf_op jit(solution)/shard_map/div | solution.py:708
  (2 shorter events, 0.1 us)
Async XLA Ops:
  26.8 30.2 %copy-start = (s32[15,32768]{1,0:T(8,128)S(1)}, s32[15,32768]{1,0:T(8,128)}, u32[]{:S(2)}) copy-start(s32[15,32768]{1,0:T(8,128)} %refs_2_.1) | copy-start | bytes 5898244
  26.8 30.2 %copy-start.1 = (s32[4096]{0:T(1024)S(1)}, s32[4096]{0:T(1024)}, u32[]{:S(2)}) copy-start(s32[4096]{0:T(1024)} %param.5) | copy-start | bytes 49156
  26.8 30.2 %copy-start.2 = (s32[4096]{0:T(1024)S(1)}, s32[4096]{0:T(1024)}, u32[]{:S(2)}) copy-start(s32[4096]{0:T(1024)} %param.6) | copy-start | bytes 49156
  44.7 12.3 %all-to-all-start.5 = ((f32[8,4,256]{2,1,0:T(4,128)}), f32[8,4,256]{2,1,0:T(4,128)S(1)}, u32[]{:S(2)}, u32[]{:S(2)}) async-start(f32[8,4,256]{2,1,0:T(4,128)} %broadcast_in_dim.4), calls=%async_computation.5 | async-start | bytes 65536 | tf_op jit(solution)/shard_map/all_to_all | solution.py:689

commit v4 on v3

--- a/solution.py
+++ b/solution.py
@@ -29,7 +29,6 @@
 MESSAGE = 8
 HALF = LANES // 2
 NONE = 255.0
-NOBODY = 4095.0
 SPOT = HALF + 16
 VMEM_BYTES = 48 << 20
 COUNT = jnp.bfloat16
@@ -355,29 +354,38 @@
         later_links += hot(later == sessions)
     weights = earlier_links + later_links
 
-    held = jnp.zeros((ROWS, LANES), jnp.float32)
-    item_row = iota((ROWS, LANES), 0)
+    one, none = jnp.ones((), jnp.bfloat16), jnp.zeros((), jnp.bfloat16)
+    item_codes = jnp.minimum(items, 255).astype(jnp.float32).astype(jnp.bfloat16)
+    row_ids = iota((ROWS, LANES), 0, jnp.float32).astype(jnp.bfloat16)
     for r in range(SLAB_ROWS):
-        same = items[r : r + 1] == item_row
-        held += jnp.where(same, weights[r : r + 1], 0.0)
-        one_hots[:, pl.ds(r * LANES, LANES)] = hot(same).astype(jnp.bfloat16)
-    margin = jnp.sum(held.T, axis=0, keepdims=True)
+        same = item_codes[r : r + 1] == row_ids
+        one_hots[:, pl.ds(r * LANES, LANES)] = jnp.where(same, one, none)
+        pair_rows[pl.ds(ROWS, 16), pl.ds(r * LANES, LANES)] = jnp.broadcast_to(
+            weights[r : r + 1], (16, LANES)
+        ).astype(jnp.bfloat16)
     total = jnp.sum(weights, axis=0, keepdims=True)
-    first_link = iota(shape, 1, jnp.float32) - earlier_links
-    place = iota((2 * LANES, LANES), 0, jnp.float32) - LANES
-    self_place = iota((2 * LANES, LANES), 1, jnp.float32)
-    sooner = place < self_place
+    first_link = (iota(shape, 1, jnp.float32) - earlier_links).astype(jnp.bfloat16)
+    place = iota((LANES, LANES), 0, jnp.float32).astype(jnp.bfloat16)
+    sooner = iota((LANES, LANES), 0) < iota((LANES, LANES), 1)
+    sooner = jnp.where(sooner, place, jnp.full((), -64.0, jnp.bfloat16))
+    last = (iota((16, LANES), 0, jnp.float32) - 16.0).astype(jnp.bfloat16)
+    no_links = jnp.zeros((LANES - 16, LANES), jnp.bfloat16)
     for r in range(SLAB_ROWS):
-        links = hot(sooner & (place >= first_link[r : r + 1])).astype(jnp.bfloat16)
+        begin = first_link[r : r + 1]
+        links = jnp.where(sooner >= begin, one, none)
         if r == 0:
-            pairs = jnp.dot(one_hots[:, pl.ds(0, LANES)], links[LANES:], preferred_element_type=jnp.float32)
+            pairs = jnp.dot(one_hots[:, pl.ds(0, LANES)], links, preferred_element_type=jnp.float32)
         else:
+            links = jnp.concatenate([no_links, jnp.where(last >= begin, one, none), links], axis=0)
             pairs = jnp.dot(
                 one_hots[:, pl.ds((r - 1) * LANES, 2 * LANES)], links, preferred_element_type=jnp.float32
             )
-        pair_rows[:, pl.ds(r * LANES, LANES)] = pairs.astype(jnp.bfloat16)
+        pair_rows[pl.ds(0, ROWS), pl.ds(r * LANES, LANES)] = pairs.astype(jnp.bfloat16)
     ordered = nt_dot(pair_rows[...], one_hots[...])
+    margin = ordered[ROWS : ROWS + 1]
+    ordered = ordered[:ROWS]
     row_pairs = ordered + ordered.T
+    item_row = iota((ROWS, LANES), 0)
 
     before = pltpu.roll(jnp.where(lane == LANES - 1, above, sessions), 1, 1)
     value = jnp.minimum(items, ROWS) + 1
@@ -439,12 +447,14 @@
     high = got[:, 2 * LANES : 3 * LANES] - target
     ordinal = ((number & (QUOTA - 1)) + 1).astype(jnp.float32)
     chosen = (got[:, :LANES] == ordinal) & (high >= 0.0) & (high < 4.0)
-    ident = got[:, LANES : 2 * LANES] + 256.0 * high
-    column = NOBODY + jnp.sum(jnp.where(chosen, ident - NOBODY, 0.0), axis=1, keepdims=True)
-    at_lane = jnp.sum(jnp.where(chosen, lanes, 0), axis=1, keepdims=True)
-    in_left = at_lane < HALF
-    index = (at_lane + jnp.where(in_left, 32 - WINDOW, -32 - WINDOW) + lanes) & (LANES - 1)
-    reach = jnp.where(in_left, got[:, 3 * LANES : 4 * LANES], got[:, 4 * LANES :])
+    ident = got[:, LANES : 2 * LANES] + 256.0 * high + 1.0
+    found = jnp.sum(
+        jnp.where(chosen, ident * LANES + lanes.astype(jnp.float32), 0.0), axis=1, keepdims=True
+    ).astype(jnp.int32)
+    column = (((found >> 7) - 1) & 4095).astype(jnp.float32)
+    at_lane = found & (LANES - 1)
+    index = ((at_lane & (HALF - 1)) + (32 - WINDOW) + lanes) & (LANES - 1)
+    reach = jnp.where(at_lane < HALF, got[:, 3 * LANES : 4 * LANES], got[:, 4 * LANES :])
     window = jnp.take_along_axis(reach, index, axis=1, mode="promise_in_bounds")
     from_lane, to_lane = iota((LANES, LANES), 0), iota((LANES, LANES), 1)
     ahead = (to_lane > WINDOW) & (from_lane > WINDOW) & (from_lane <= to_lane)
@@ -644,7 +654,7 @@
             pltpu.VMEM((LANES, 5 * LANES), jnp.bfloat16),
             pltpu.VMEM((SLABS * QUOTA, LANES), jnp.int32),
             pltpu.VMEM((ROWS, SLAB_ROWS * LANES), jnp.bfloat16),
-            pltpu.VMEM((ROWS, SLAB_ROWS * LANES), jnp.bfloat16),
+            pltpu.VMEM((ROWS + 16, SLAB_ROWS * LANES), jnp.bfloat16),
             pltpu.SemaphoreType.DMA((2,)),
         ],
         compiler_params=pltpu.CompilerParams(vmem_limit_bytes=VMEM_BYTES),

time: 58.3 us -> 57.3 us (0.983)
  Pallas kernels: 10.1 us -> 9.2 us
    pallas_call x1, Pallas kernels: 5.59 us -> 4.65 us  [route(): pl.pallas_call(lambda *refs: route_kernel(where, *refs), out_shape=jax.Sh...]
where the time goes in v4:
time: 57.3 us; the launch traced here: 56.9 us
  blocking collectives  33.9 us (59%)
  Pallas kernels  9.2 us (16%)
  starting transfers between devices  7.53 us (13%)
  waiting for transfers between devices  4.07 us (7%)
  between operations  0.69 us (1%)
  other arithmetic  0.66 us (1%)
  local copies, waits for them, and re-layouts  0.62 us (1%)
    all_to_all x1, blocking collectives, local(): lax.all_to_all(route(where, items, sessions), 'stream', 0, 0, tiled=True)  21.2 us
    all_to_all x1, blocking collectives, shares(): rows = jnp.sum(lax.all_to_all(part, 'stream', 0, 0, tiled=True), axis=0)  12.7 us
    all_to_all x1, starting transfers between devices, shares(): return lax.all_to_all(spread, 'item', 0, 0, tiled=True)  7.53 us
    pallas_call x1, Pallas kernels, route(): pl.pallas_call(lambda *refs: route_kernel(where, *refs), out_shape=jax.Sh...  4.65 us
    pallas_call x1, Pallas kernels, sketch_part(): pl.pallas_call(lambda *refs: sketch_kernel(where, *refs), out_shape=(jax....  4.55 us
    all_to_all x1, waiting for transfers between devices, shares(): return lax.all_to_all(spread, 'item', 0, 0, tiled=True)  4.07 us
  transfers between devices with their start and end apart: 1, of which 1 were waited for; matrix products, arithmetic and copies ran while one was open for 0% of the time, Pallas kernels for 0%

profile of v4, /device:TPU:1, one launch (start us, length us, event | category | flops | bytes accessed | tf_op | source)
XLA Modules:
  0.0 56.9 jit_solution(13547635119578740163)
XLA Ops:
  0.0 4.6 %route_events.1 = s32[32,8,128]{2,1,0:T(8,128)S(1)} custom-call(s32[32,128]{1,0:T(8,128)} %bitcast.3, s32[32,128]{1,0:T(8,128)} %bitcast.5), custom_call_target="tpu_custom_call" | custom-call | tf_op jit(solution)/shard_map/route_events/pallas_call | solution.py:645
  4.7 21.2 %all_to_all.33.refs_0_ = s32[32,8,128]{2,1,0:T(8,128)S(1)} all-to-all(s32[32,8,128]{2,1,0:T(8,128)S(1)} %route_events.1), channel_id=1, replica_groups=mesh['stream'=32,'item'=8] {'stream'}, dimensions={0} | all-to-all | bytes 262144 | tf_op jit(solution)/shard_map/all_to_all | solution.py:715
  25.8 0.0 copy-start
  25.8 0.0 copy-start.1
  25.8 0.0 copy-start.2
  25.8 4.6 %sketch_part.1 = (f32[32,4,256]{2,1,0:T(4,128)S(1)}, s32[1,1]{1,0:T(1,128)}) custom-call(s32[32,8,128]{2,1,0:T(8,128)S(1)} %all_to_all.33.refs_0_, s32[15,32768]{1,0:T(8,128)} %refs_2_.1, s32[15,32768]{1,0:T(8,128)} %refs_2_.1), custom_call_target="tpu_custom_call" | custom-call | tf_op jit(solution)/shard_map/sketch_part/pallas_call | solution.py:667
  30.4 12.7 %all_to_all.34 = f32[32,4,256]{2,1,0:T(4,128)S(1)} all-to-all(f32[32,4,256]{2,1,0:T(4,128)S(1)} %get-tuple-element.27), channel_id=1, replica_groups=mesh['stream'=32,'item'=8] {'stream'}, dimensions={0} | all-to-all | bytes 262144 | tf_op jit(solution)/shard_map/all_to_all | solution.py:697
  43.2 0.6 %broadcast_in_dim.4 = f32[8,4,256]{2,1,0:T(4,128)} broadcast(f32[4,256]{1,0:T(4,128)S(1)} %reduce_sum.33), dimensions={1,2} | broadcast | bytes 36864 | tf_op jit(solution)/shard_map/broadcast_in_dim | solution.py:698
  43.8 7.5 %all-to-all-start.5 = ((f32[8,4,256]{2,1,0:T(4,128)}), f32[8,4,256]{2,1,0:T(4,128)S(1)}, u32[]{:S(2)}, u32[]{:S(2)}) async-start(f32[8,4,256]{2,1,0:T(4,128)} %broadcast_in_dim.4), calls=%async_computation.5 | async-start | bytes 65536 | tf_op jit(solution)/shard_map/all_to_all | solution.py:699
  52.0 4.1 %all-to-all-done.5 = f32[8,4,256]{2,1,0:T(4,128)S(1)} async-done(((f32[8,4,256]{2,1,0:T(4,128)}), f32[8,4,256]{2,1,0:T(4,128)S(1)}, u32[]{:S(2)}, u32[]{:S(2)}) %all-to-all-start.5) | async-done | bytes 32800 | tf_op jit(solution)/shard_map/all_to_all | solution.py:699
  56.0 0.0 copy-done
  56.0 0.0 copy-done.1
  56.1 0.0 copy-done.2
  56.1 0.3 conditional.1
  56.3 0.6 %broadcast_multiply_fusion = f32[4,256]{1,0:T(4,128)} fusion(f32[4,256]{1,0:T(4,128)S(1)} %get-tuple-element.28), kind=kLoop, calls=%fused_computation | loop fusion | flops 1024 | bytes 8192 | tf_op jit(solution)/shard_map/div | solution.py:718
  (2 shorter events, 0.1 us)
Async XLA Ops:
  25.8 30.2 %copy-start = (s32[15,32768]{1,0:T(8,128)S(1)}, s32[15,32768]{1,0:T(8,128)}, u32[]{:S(2)}) copy-start(s32[15,32768]{1,0:T(8,128)} %refs_2_.1) | copy-start | bytes 5898244
  25.8 30.2 %copy-start.1 = (s32[4096]{0:T(1024)S(1)}, s32[4096]{0:T(1024)}, u32[]{:S(2)}) copy-start(s32[4096]{0:T(1024)} %param.5) | copy-start | bytes 49156
  25.8 30.2 %copy-start.2 = (s32[4096]{0:T(1024)S(1)}, s32[4096]{0:T(1024)}, u32[]{:S(2)}) copy-start(s32[4096]{0:T(1024)} %param.6) | copy-start | bytes 49156
  43.8 12.2 %all-to-all-start.5 = ((f32[8,4,256]{2,1,0:T(4,128)}), f32[8,4,256]{2,1,0:T(4,128)S(1)}, u32[]{:S(2)}, u32[]{:S(2)}) async-start(f32[8,4,256]{2,1,0:T(4,128)} %broadcast_in_dim.4), calls=%async_computation.5 | async-start | bytes 65536 | tf_op jit(solution)/shard_map/all_to_all | solution.py:699

commit v5 on v4

--- a/solution.py
+++ b/solution.py
@@ -369,6 +369,7 @@
     sooner = iota((LANES, LANES), 0) < iota((LANES, LANES), 1)
     sooner = jnp.where(sooner, place, jnp.full((), -64.0, jnp.bfloat16))
     last = (iota((16, LANES), 0, jnp.float32) - 16.0).astype(jnp.bfloat16)
+    ordered = jnp.zeros((ROWS + 16, ROWS), jnp.float32)
     no_links = jnp.zeros((LANES - 16, LANES), jnp.bfloat16)
     for r in range(SLAB_ROWS):
         begin = first_link[r : r + 1]
@@ -381,7 +382,9 @@
                 one_hots[:, pl.ds((r - 1) * LANES, 2 * LANES)], links, preferred_element_type=jnp.float32
             )
         pair_rows[pl.ds(0, ROWS), pl.ds(r * LANES, LANES)] = pairs.astype(jnp.bfloat16)
-    ordered = nt_dot(pair_rows[...], one_hots[...])
+        if r % 4 == 3:
+            ready = pl.ds((r - 3) * LANES, 4 * LANES)
+            ordered += nt_dot(pair_rows[:, ready], one_hots[:, ready])
     margin = ordered[ROWS : ROWS + 1]
     ordered = ordered[:ROWS]
     row_pairs = ordered + ordered.T
@@ -618,8 +621,15 @@
     margin_high = jnp.sum(got_ref[:, 5, :], axis=0, keepdims=True)
     margins = jnp.where(item_lane[:1] < HALF, pltpu.roll(margin_low, HALF, 1), margin_high)
     held = jnp.where(item_row == item_lane, margins.astype(jnp.float32), 0.0)
-    for s in range(SLABS):
-        held += jnp.where(items[s : s + 1] == item_row, cross[s : s + 1], 0.0)
+    edge_codes = jnp.minimum(items, 255).astype(jnp.float32).astype(jnp.bfloat16)
+    edge_rows = item_row.astype(jnp.float32).astype(jnp.bfloat16)
+    edge_cross = cross.astype(jnp.bfloat16)
+    for first in range(0, SLABS, 16):
+        part = jnp.zeros((ROWS, LANES), jnp.bfloat16)
+        for s in range(first, first + 16):
+            same = edge_codes[s : s + 1] == edge_rows
+            part += jnp.where(same, edge_cross[s : s + 1], jnp.zeros((), jnp.bfloat16))
+        held += part.astype(jnp.float32)
     row_margin = jnp.sum(held, axis=1, keepdims=True)
     totals = jnp.where(lane == SPOT, raw_items, 0).astype(jnp.float32) + cross
     pair_total = jnp.sum(jnp.sum(totals, axis=0, keepdims=True), axis=1, keepdims=True)

time: 57.3 us -> 56.2 us (0.981)
  Pallas kernels: 9.2 us -> 8.29 us
    pallas_call x1, Pallas kernels: 4.65 us -> 3.93 us  [route(): pl.pallas_call(lambda *refs: route_kernel(where, *refs), out_shape=jax.Sh...]
where the time goes in v5:
time: 56.2 us; the launch traced here: 55.8 us
  blocking collectives  33.8 us (60%)
  Pallas kernels  8.29 us (15%)
  starting transfers between devices  7.63 us (14%)
  waiting for transfers between devices  4.07 us (7%)
  between operations  0.69 us (1%)
  other arithmetic  0.66 us (1%)
  local copies, waits for them, and re-layouts  0.62 us (1%)
    all_to_all x1, blocking collectives, local(): lax.all_to_all(route(where, items, sessions), 'stream', 0, 0, tiled=True)  21.2 us
    all_to_all x1, blocking collectives, shares(): rows = jnp.sum(lax.all_to_all(part, 'stream', 0, 0, tiled=True), axis=0)  12.6 us
    all_to_all x1, starting transfers between devices, shares(): return lax.all_to_all(spread, 'item', 0, 0, tiled=True)  7.63 us
    pallas_call x1, Pallas kernels, sketch_part(): pl.pallas_call(lambda *refs: sketch_kernel(where, *refs), out_shape=(jax....  4.36 us
    all_to_all x1, waiting for transfers between devices, shares(): return lax.all_to_all(spread, 'item', 0, 0, tiled=True)  4.07 us
    pallas_call x1, Pallas kernels, route(): pl.pallas_call(lambda *refs: route_kernel(where, *refs), out_shape=jax.Sh...  3.93 us
  transfers between devices with their start and end apart: 1, of which 1 were waited for; matrix products, arithmetic and copies ran while one was open for 0% of the time, Pallas kernels for 0%

profile of v5, /device:TPU:1, one launch (start us, length us, event | category | flops | bytes accessed | tf_op | source)
XLA Modules:
  0.0 55.8 jit_solution(10073871906471544523)
XLA Ops:
  0.0 3.9 %route_events.1 = s32[32,8,128]{2,1,0:T(8,128)S(1)} custom-call(s32[32,128]{1,0:T(8,128)} %bitcast.3, s32[32,128]{1,0:T(8,128)} %bitcast.5), custom_call_target="tpu_custom_call" | custom-call | tf_op jit(solution)/shard_map/route_events/pallas_call | solution.py:655
  3.9 21.2 %all_to_all.33.refs_0_ = s32[32,8,128]{2,1,0:T(8,128)S(1)} all-to-all(s32[32,8,128]{2,1,0:T(8,128)S(1)} %route_events.1), channel_id=1, replica_groups=mesh['stream'=32,'item'=8] {'stream'}, dimensions={0} | all-to-all | bytes 262144 | tf_op jit(solution)/shard_map/all_to_all | solution.py:725
  25.1 0.0 copy-start
  25.1 0.0 copy-start.1
  25.1 0.0 copy-start.2
  25.1 4.4 %sketch_part.1 = (f32[32,4,256]{2,1,0:T(4,128)S(1)}, s32[1,1]{1,0:T(1,128)}) custom-call(s32[32,8,128]{2,1,0:T(8,128)S(1)} %all_to_all.33.refs_0_, s32[15,32768]{1,0:T(8,128)} %refs_2_.1, s32[15,32768]{1,0:T(8,128)} %refs_2_.1), custom_call_target="tpu_custom_call" | custom-call | tf_op jit(solution)/shard_map/sketch_part/pallas_call | solution.py:677
  29.5 12.6 %all_to_all.34 = f32[32,4,256]{2,1,0:T(4,128)S(1)} all-to-all(f32[32,4,256]{2,1,0:T(4,128)S(1)} %get-tuple-element.27), channel_id=1, replica_groups=mesh['stream'=32,'item'=8] {'stream'}, dimensions={0} | all-to-all | bytes 262144 | tf_op jit(solution)/shard_map/all_to_all | solution.py:707
  42.2 0.6 %broadcast_in_dim.4 = f32[8,4,256]{2,1,0:T(4,128)} broadcast(f32[4,256]{1,0:T(4,128)S(1)} %reduce_sum.33), dimensions={1,2} | broadcast | bytes 36864 | tf_op jit(solution)/shard_map/broadcast_in_dim | solution.py:708
  42.8 7.6 %all-to-all-start.5 = ((f32[8,4,256]{2,1,0:T(4,128)}), f32[8,4,256]{2,1,0:T(4,128)S(1)}, u32[]{:S(2)}, u32[]{:S(2)}) async-start(f32[8,4,256]{2,1,0:T(4,128)} %broadcast_in_dim.4), calls=%async_computation.5 | async-start | bytes 65536 | tf_op jit(solution)/shard_map/all_to_all | solution.py:709
  51.1 4.1 %all-to-all-done.5 = f32[8,4,256]{2,1,0:T(4,128)S(1)} async-done(((f32[8,4,256]{2,1,0:T(4,128)}), f32[8,4,256]{2,1,0:T(4,128)S(1)}, u32[]{:S(2)}, u32[]{:S(2)}) %all-to-all-start.5) | async-done | bytes 32800 | tf_op jit(solution)/shard_map/all_to_all | solution.py:709
  55.1 0.0 copy-done
  55.1 0.0 copy-done.1
  55.1 0.0 copy-done.2
  55.2 0.6 %broadcast_multiply_fusion = f32[4,256]{1,0:T(4,128)} fusion(f32[4,256]{1,0:T(4,128)S(1)} %get-tuple-element.28), kind=kLoop, calls=%fused_computation | loop fusion | flops 1024 | bytes 8192 | tf_op jit(solution)/shard_map/div | solution.py:728
  (3 shorter events, 0.1 us)
Async XLA Ops:
  25.1 30.0 %copy-start = (s32[15,32768]{1,0:T(8,128)S(1)}, s32[15,32768]{1,0:T(8,128)}, u32[]{:S(2)}) copy-start(s32[15,32768]{1,0:T(8,128)} %refs_2_.1) | copy-start | bytes 5898244
  25.1 30.0 %copy-start.1 = (s32[4096]{0:T(1024)S(1)}, s32[4096]{0:T(1024)}, u32[]{:S(2)}) copy-start(s32[4096]{0:T(1024)} %param.5) | copy-start | bytes 49156
  25.1 30.0 %copy-start.2 = (s32[4096]{0:T(1024)S(1)}, s32[4096]{0:T(1024)}, u32[]{:S(2)}) copy-start(s32[4096]{0:T(1024)} %param.6) | copy-start | bytes 49156
  42.8 12.4 %all-to-all-start.5 = ((f32[8,4,256]{2,1,0:T(4,128)}), f32[8,4,256]{2,1,0:T(4,128)S(1)}, u32[]{:S(2)}, u32[]{:S(2)}) async-start(f32[8,4,256]{2,1,0:T(4,128)} %broadcast_in_dim.4), calls=%async_computation.5 | async-start | bytes 65536 | tf_op jit(solution)/shard_map/all_to_all | solution.py:709

commit v6 on v5

--- a/solution.py
+++ b/solution.py
@@ -382,8 +382,8 @@
                 one_hots[:, pl.ds((r - 1) * LANES, 2 * LANES)], links, preferred_element_type=jnp.float32
             )
         pair_rows[pl.ds(0, ROWS), pl.ds(r * LANES, LANES)] = pairs.astype(jnp.bfloat16)
-        if r % 4 == 3:
-            ready = pl.ds((r - 3) * LANES, 4 * LANES)
+        if r % 8 == 7:
+            ready = pl.ds((r - 7) * LANES, 8 * LANES)
             ordered += nt_dot(pair_rows[:, ready], one_hots[:, ready])
     margin = ordered[ROWS : ROWS + 1]
     ordered = ordered[:ROWS]
@@ -587,15 +587,13 @@
 
     windows = got_ref[...].reshape(SLABS * MESSAGE, LANES).T[:HALF]
     low, high = (windows & 4095).astype(jnp.float32), (windows >> 12).astype(jnp.float32)
-    blocks, idents = [], []
+    within = first_crossed[:, :OWNED]
     for g in range(QUOTA // 8):
         near = jnp.concatenate([low[16 * g : 16 * g + 16], high[16 * g : 16 * g + 16]], axis=0)
-        idents.append(near[WINDOW : WINDOW + 1])
-        blocks.append(count_pairs(near, (WINDOW, 31)))
-    ident = jnp.concatenate(idents, axis=1)
-    pairs = jnp.concatenate(blocks, axis=1)
-    column_hot = hot(ident == iota((OWNED, ident.shape[1]), 0, jnp.float32)).astype(jnp.bfloat16)
-    counts[:, pl.ds(0, OWNED)] = nt_dot(pairs, column_hot) + first_crossed[:, :OWNED]
+        ident = near[WINDOW : WINDOW + 1]
+        column_hot = hot(ident == iota((OWNED, ident.shape[1]), 0, jnp.float32)).astype(jnp.bfloat16)
+        within += nt_dot(count_pairs(near, (WINDOW, 31)), column_hot)
+    counts[:, pl.ds(0, OWNED)] = within
 
     low_sum = jnp.zeros((MESSAGE, LANES), jnp.int32)
     high_sum = jnp.zeros((MESSAGE, LANES), jnp.int32)

time: 56.2 us -> 55.9 us (level)
  no operation moved by 1% of the time
where the time goes in v6:
time: 55.9 us; the launch traced here: 55.5 us
  blocking collectives  33.8 us (60%)
  Pallas kernels  8.04 us (14%)
  starting transfers between devices  7.62 us (14%)
  waiting for transfers between devices  4.07 us (7%)
  between operations  0.69 us (1%)
  other arithmetic  0.66 us (1%)
  local copies, waits for them, and re-layouts  0.62 us (1%)
    all_to_all x1, blocking collectives, local(): lax.all_to_all(route(where, items, sessions), 'stream', 0, 0, tiled=True)  21.2 us
    all_to_all x1, blocking collectives, shares(): rows = jnp.sum(lax.all_to_all(part, 'stream', 0, 0, tiled=True), axis=0)  12.6 us
    all_to_all x1, starting transfers between devices, shares(): return lax.all_to_all(spread, 'item', 0, 0, tiled=True)  7.62 us
    pallas_call x1, Pallas kernels, sketch_part(): pl.pallas_call(lambda *refs: sketch_kernel(where, *refs), out_shape=(jax....  4.24 us
    all_to_all x1, waiting for transfers between devices, shares(): return lax.all_to_all(spread, 'item', 0, 0, tiled=True)  4.07 us
    pallas_call x1, Pallas kernels, route(): pl.pallas_call(lambda *refs: route_kernel(where, *refs), out_shape=jax.Sh...  3.81 us
  transfers between devices with their start and end apart: 1, of which 1 were waited for; matrix products, arithmetic and copies ran while one was open for 0% of the time, Pallas kernels for 0%

profile of v6, /device:TPU:1, one launch (start us, length us, event | category | flops | bytes accessed | tf_op | source)
XLA Modules:
  0.0 55.5 jit_solution(14827964832548666056)
XLA Ops:
  0.0 3.8 %route_events.1 = s32[32,8,128]{2,1,0:T(8,128)S(1)} custom-call(s32[32,128]{1,0:T(8,128)} %bitcast.3, s32[32,128]{1,0:T(8,128)} %bitcast.5), custom_call_target="tpu_custom_call" | custom-call | tf_op jit(solution)/shard_map/route_events/pallas_call | solution.py:653
  3.8 21.2 %all_to_all.33.refs_0_ = s32[32,8,128]{2,1,0:T(8,128)S(1)} all-to-all(s32[32,8,128]{2,1,0:T(8,128)S(1)} %route_events.1), channel_id=1, replica_groups=mesh['stream'=32,'item'=8] {'stream'}, dimensions={0} | all-to-all | bytes 262144 | tf_op jit(solution)/shard_map/all_to_all | solution.py:723
  25.0 0.0 copy-start
  25.0 0.0 copy-start.1
  25.0 0.0 copy-start.2
  25.0 4.2 %sketch_part.1 = (f32[32,4,256]{2,1,0:T(4,128)S(1)}, s32[1,1]{1,0:T(1,128)}) custom-call(s32[32,8,128]{2,1,0:T(8,128)S(1)} %all_to_all.33.refs_0_, s32[15,32768]{1,0:T(8,128)} %refs_2_.1, s32[15,32768]{1,0:T(8,128)} %refs_2_.1), custom_call_target="tpu_custom_call" | custom-call | tf_op jit(solution)/shard_map/sketch_part/pallas_call | solution.py:675
  29.2 12.6 %all_to_all.34 = f32[32,4,256]{2,1,0:T(4,128)S(1)} all-to-all(f32[32,4,256]{2,1,0:T(4,128)S(1)} %get-tuple-element.27), channel_id=1, replica_groups=mesh['stream'=32,'item'=8] {'stream'}, dimensions={0} | all-to-all | bytes 262144 | tf_op jit(solution)/shard_map/all_to_all | solution.py:705
  41.9 0.6 %broadcast_in_dim.4 = f32[8,4,256]{2,1,0:T(4,128)} broadcast(f32[4,256]{1,0:T(4,128)S(1)} %reduce_sum.33), dimensions={1,2} | broadcast | bytes 36864 | tf_op jit(solution)/shard_map/broadcast_in_dim | solution.py:706
  42.5 7.6 %all-to-all-start.5 = ((f32[8,4,256]{2,1,0:T(4,128)}), f32[8,4,256]{2,1,0:T(4,128)S(1)}, u32[]{:S(2)}, u32[]{:S(2)}) async-start(f32[8,4,256]{2,1,0:T(4,128)} %broadcast_in_dim.4), calls=%async_computation.5 | async-start | bytes 65536 | tf_op jit(solution)/shard_map/all_to_all | solution.py:707
  50.8 4.1 %all-to-all-done.5 = f32[8,4,256]{2,1,0:T(4,128)S(1)} async-done(((f32[8,4,256]{2,1,0:T(4,128)}), f32[8,4,256]{2,1,0:T(4,128)S(1)}, u32[]{:S(2)}, u32[]{:S(2)}) %all-to-all-start.5) | async-done | bytes 32800 | tf_op jit(solution)/shard_map/all_to_all | solution.py:707
  54.9 0.0 copy-done
  54.9 0.0 copy-done.1
  54.9 0.0 copy-done.2
  54.9 0.6 %broadcast_multiply_fusion = f32[4,256]{1,0:T(4,128)} fusion(f32[4,256]{1,0:T(4,128)S(1)} %get-tuple-element.28), kind=kLoop, calls=%fused_computation | loop fusion | flops 1024 | bytes 8192 | tf_op jit(solution)/shard_map/div | solution.py:726
  (3 shorter events, 0.1 us)
Async XLA Ops:
  25.0 29.9 %copy-start = (s32[15,32768]{1,0:T(8,128)S(1)}, s32[15,32768]{1,0:T(8,128)}, u32[]{:S(2)}) copy-start(s32[15,32768]{1,0:T(8,128)} %refs_2_.1) | copy-start | bytes 5898244
  25.0 29.9 %copy-start.1 = (s32[4096]{0:T(1024)S(1)}, s32[4096]{0:T(1024)}, u32[]{:S(2)}) copy-start(s32[4096]{0:T(1024)} %param.5) | copy-start | bytes 49156
  25.0 29.9 %copy-start.2 = (s32[4096]{0:T(1024)S(1)}, s32[4096]{0:T(1024)}, u32[]{:S(2)}) copy-start(s32[4096]{0:T(1024)} %param.6) | copy-start | bytes 49156
  42.5 12.3 %all-to-all-start.5 = ((f32[8,4,256]{2,1,0:T(4,128)}), f32[8,4,256]{2,1,0:T(4,128)S(1)}, u32[]{:S(2)}, u32[]{:S(2)}) async-start(f32[8,4,256]{2,1,0:T(4,128)} %broadcast_in_dim.4), calls=%async_computation.5 | async-start | bytes 65536 | tf_op jit(solution)/shard_map/all_to_all | solution.py:707

commit v7 on v6

--- a/solution.py
+++ b/solution.py
@@ -438,9 +438,11 @@
     ]
     for k, field in enumerate(fields):
         table[pl.ds(0, SLAB_ROWS), pl.ds(k * LANES, LANES)] = field.astype(jnp.bfloat16)
-    slot = iota((QUOTA, LANES), 0, jnp.float32)
+    slot = iota((QUOTA, LANES), 0, jnp.float32).astype(jnp.bfloat16)
+    from_slot = jnp.minimum(starts, 255.0).astype(jnp.bfloat16)
+    to_slot = jnp.minimum(ends, 255.0).astype(jnp.bfloat16)
     picks = [
-        hot((slot >= starts[s : s + 1]) & (slot < ends[s : s + 1])).astype(jnp.bfloat16)
+        jnp.where((slot >= from_slot[s : s + 1]) & (slot < to_slot[s : s + 1]), one, none)
         for s in range(SLABS)
     ]
     got = jnp.dot(jnp.concatenate(picks, axis=0), table[...], preferred_element_type=jnp.float32)

time: 55.9 us -> 55.9 us (level)
  no operation moved by 1% of the time
where the time goes in v7:
time: 55.9 us; the launch traced here: 55.5 us
  blocking collectives  33.8 us (60%)
  Pallas kernels  8.03 us (14%)
  starting transfers between devices  7.63 us (14%)
  waiting for transfers between devices  4.07 us (7%)
  between operations  0.69 us (1%)
  other arithmetic  0.66 us (1%)
  local copies, waits for them, and re-layouts  0.62 us (1%)
    all_to_all x1, blocking collectives, local(): lax.all_to_all(route(where, items, sessions), 'stream', 0, 0, tiled=True)  21.2 us
    all_to_all x1, blocking collectives, shares(): rows = jnp.sum(lax.all_to_all(part, 'stream', 0, 0, tiled=True), axis=0)  12.6 us
    all_to_all x1, starting transfers between devices, shares(): return lax.all_to_all(spread, 'item', 0, 0, tiled=True)  7.63 us
    pallas_call x1, Pallas kernels, sketch_part(): pl.pallas_call(lambda *refs: sketch_kernel(where, *refs), out_shape=(jax....  4.23 us
    all_to_all x1, waiting for transfers between devices, shares(): return lax.all_to_all(spread, 'item', 0, 0, tiled=True)  4.07 us
    pallas_call x1, Pallas kernels, route(): pl.pallas_call(lambda *refs: route_kernel(where, *refs), out_shape=jax.Sh...  3.79 us
  transfers between devices with their start and end apart: 1, of which 1 were waited for; matrix products, arithmetic and copies ran while one was open for 0% of the time, Pallas kernels for 0%

profile of v7, /device:TPU:1, one launch (start us, length us, event | category | flops | bytes accessed | tf_op | source)
XLA Modules:
  0.0 55.5 jit_solution(4549081070768078808)
XLA Ops:
  0.0 3.8 %route_events.1 = s32[32,8,128]{2,1,0:T(8,128)S(1)} custom-call(s32[32,128]{1,0:T(8,128)} %bitcast.3, s32[32,128]{1,0:T(8,128)} %bitcast.5), custom_call_target="tpu_custom_call" | custom-call | tf_op jit(solution)/shard_map/route_events/pallas_call | solution.py:655
  3.8 21.2 %all_to_all.33.refs_0_ = s32[32,8,128]{2,1,0:T(8,128)S(1)} all-to-all(s32[32,8,128]{2,1,0:T(8,128)S(1)} %route_events.1), channel_id=1, replica_groups=mesh['stream'=32,'item'=8] {'stream'}, dimensions={0} | all-to-all | bytes 262144 | tf_op jit(solution)/shard_map/all_to_all | solution.py:725
  25.0 0.0 copy-start
  25.0 0.0 copy-start.1
  25.0 0.0 copy-start.2
  25.0 4.2 %sketch_part.1 = (f32[32,4,256]{2,1,0:T(4,128)S(1)}, s32[1,1]{1,0:T(1,128)}) custom-call(s32[32,8,128]{2,1,0:T(8,128)S(1)} %all_to_all.33.refs_0_, s32[15,32768]{1,0:T(8,128)} %refs_2_.1, s32[15,32768]{1,0:T(8,128)} %refs_2_.1), custom_call_target="tpu_custom_call" | custom-call | tf_op jit(solution)/shard_map/sketch_part/pallas_call | solution.py:677
  29.2 12.6 %all_to_all.34 = f32[32,4,256]{2,1,0:T(4,128)S(1)} all-to-all(f32[32,4,256]{2,1,0:T(4,128)S(1)} %get-tuple-element.27), channel_id=1, replica_groups=mesh['stream'=32,'item'=8] {'stream'}, dimensions={0} | all-to-all | bytes 262144 | tf_op jit(solution)/shard_map/all_to_all | solution.py:707
  41.9 0.6 %broadcast_in_dim.4 = f32[8,4,256]{2,1,0:T(4,128)} broadcast(f32[4,256]{1,0:T(4,128)S(1)} %reduce_sum.33), dimensions={1,2} | broadcast | bytes 36864 | tf_op jit(solution)/shard_map/broadcast_in_dim | solution.py:708
  42.5 7.6 %all-to-all-start.5 = ((f32[8,4,256]{2,1,0:T(4,128)}), f32[8,4,256]{2,1,0:T(4,128)S(1)}, u32[]{:S(2)}, u32[]{:S(2)}) async-start(f32[8,4,256]{2,1,0:T(4,128)} %broadcast_in_dim.4), calls=%async_computation.5 | async-start | bytes 65536 | tf_op jit(solution)/shard_map/all_to_all | solution.py:709
  50.8 4.1 %all-to-all-done.5 = f32[8,4,256]{2,1,0:T(4,128)S(1)} async-done(((f32[8,4,256]{2,1,0:T(4,128)}), f32[8,4,256]{2,1,0:T(4,128)S(1)}, u32[]{:S(2)}, u32[]{:S(2)}) %all-to-all-start.5) | async-done | bytes 32800 | tf_op jit(solution)/shard_map/all_to_all | solution.py:709
  54.9 0.0 copy-done
  54.9 0.0 copy-done.1
  54.9 0.0 copy-done.2
  54.9 0.6 %broadcast_multiply_fusion = f32[4,256]{1,0:T(4,128)} fusion(f32[4,256]{1,0:T(4,128)S(1)} %get-tuple-element.28), kind=kLoop, calls=%fused_computation | loop fusion | flops 1024 | bytes 8192 | tf_op jit(solution)/shard_map/div | solution.py:728
  (3 shorter events, 0.1 us)
Async XLA Ops:
  25.0 29.9 %copy-start = (s32[15,32768]{1,0:T(8,128)S(1)}, s32[15,32768]{1,0:T(8,128)}, u32[]{:S(2)}) copy-start(s32[15,32768]{1,0:T(8,128)} %refs_2_.1) | copy-start | bytes 5898244
  25.0 29.9 %copy-start.1 = (s32[4096]{0:T(1024)S(1)}, s32[4096]{0:T(1024)}, u32[]{:S(2)}) copy-start(s32[4096]{0:T(1024)} %param.5) | copy-start | bytes 49156
  25.0 29.9 %copy-start.2 = (s32[4096]{0:T(1024)S(1)}, s32[4096]{0:T(1024)}, u32[]{:S(2)}) copy-start(s32[4096]{0:T(1024)} %param.6) | copy-start | bytes 49156
  42.5 12.3 %all-to-all-start.5 = ((f32[8,4,256]{2,1,0:T(4,128)}), f32[8,4,256]{2,1,0:T(4,128)S(1)}, u32[]{:S(2)}, u32[]{:S(2)}) async-start(f32[8,4,256]{2,1,0:T(4,128)} %broadcast_in_dim.4), calls=%async_computation.5 | async-start | bytes 65536 | tf_op jit(solution)/shard_map/all_to_all | solution.py:709
